TPU v7x, 32 devices: a whole 2x2x4 slice. The times are simulated.
32 devices in a mesh: car: 2 (over y), branch: 4 (over x, core), pts: 4 (over z).
Axes of the slice: x: 2, y: 2, z: 4, core: 2. Of those that a mesh axis runs over, the one named last changes fastest.
Arguments:
- anchors: bfloat16 [512, 384], P(('car', 'branch', 'pts')), parts along dimension 0, may hold values from -6 to 6
- queries: bfloat16 [4096, 384], P(('car', 'branch', 'pts')), parts along dimension 0, may hold values from -6 to 6
- query_kind: int32 [4096], P(('car', 'branch', 'pts')), parts along dimension 0, may hold values from 0 to 1
- live_count: int32 [32], P(('car', 'branch', 'pts')), parts along dimension 0, may hold values from 16 to 128, as said below
- anchor_gain: float32 [384], replicated, may hold values from 0.25 to 1.75
- query_gain: float32 [384], replicated, may hold values from 0.25 to 1.75
- w_query: bfloat16 [384, 384], replicated, may hold values from -0.3125 to 0.3125
- w_key: bfloat16 [384, 384], replicated, may hold values from -0.3125 to 0.3125
- w_value: bfloat16 [384, 384], replicated, may hold values from -0.3125 to 0.3125
- w_out: bfloat16 [384, 384], replicated, may hold values from -0.3125 to 0.3125
- cotangent: bfloat16 [4096, 384], P(('car', 'branch', 'pts')), parts along dimension 0, may hold values from -6 to 6
Outputs:
- fields: bfloat16 [4096, 384], P(('car', 'branch', 'pts')), parts along dimension 0
- query_grad: float32 [4096, 384], P(('car', 'branch', 'pts')), parts along dimension 0
- anchor_grad: float32 [512, 384], P(('car', 'branch', 'pts')), parts along dimension 0
There are 2 independent parts, one for each index of `car`. A program takes and returns all parts, laid end to end along the dimension named above; an argument that names none is the same for every part. Nothing has to cross between parts.
Inputs may be any that keep to these rules, and one draw needn't show every extreme that they name: `live_count`: each entry counts used slots of one device's 128 slots, the used ones first; some device has all 128 used in every draw.
All inputs are finite; a program needn't handle non-finite values.
Results may differ from a plain program's by a relative error of at most 0.011.
Values may be sent and summed in bfloat16 or wider, within the bound.
No kernel may reach another device: no remote copies, remote signals or barrier semaphores. Data moves between devices by JAX's collectives and lax.ppermute only.
A program may use at most 64 MiB of HBM per device.

v0:
```python
import functools

import jax
import jax.numpy as jnp
from jax import lax
from jax.experimental import pallas as pl
from jax.experimental.pallas import tpu as pltpu
from jax.sharding import PartitionSpec as P


HEADS = 6
GROUP_AXES = ("branch", "pts")

NN = (((1,), (0,)), ((), ()))
NT = (((1,), (1,)), ((), ()))
TN = (((0,), (0,)), ((), ()))


def mm(a, b, dims):
    return lax.dot_general(a, b, dims, preferred_element_type=jnp.float32)


def centered(rows):
    values = rows.astype(jnp.float32)
    center = values - jnp.mean(values, axis=-1, keepdims=True)
    variance = jnp.mean(center * center, axis=-1, keepdims=True)
    return center, lax.rsqrt(variance + 1e-05)


def norm_pullback(center, scale, gain, grad):
    through = grad * gain
    inner = jnp.mean(through * center, axis=-1, keepdims=True)
    grad_center = scale * through - center * (scale * scale * scale * inner)
    return grad_center - jnp.mean(grad_center, axis=-1, keepdims=True)


def as_row(gain):
    return gain[...].reshape(1, -1)


def live_rows(count, rows):
    return (lax.broadcasted_iota(jnp.int32, (rows, 1), 0) < count).astype(jnp.float32)


def query_side(*refs):
    total = (len(refs) - 5) // 2
    sources, outs, count, sems = refs[: total + 1], refs[total + 1 : -2], refs[-2], refs[-1]
    (heads_out, grad_out, live_out), kept = outs[:3], outs[3:]
    copies = [pltpu.make_async_copy(a, b, sems.at[k]) for k, (a, b) in enumerate(zip(sources, kept + (count,)))]
    for copy in copies:
        copy.start()
    queries, cot, gain, w_query, w_out = kept[:5]
    for k in (0, 2):
        copies[k].wait()
    center, scale = centered(queries[...])
    query_normed = (center * scale * as_row(gain)).astype(jnp.bfloat16)
    copies[3].wait()
    heads_out[...] = mm(query_normed, w_query[...], NN).astype(jnp.bfloat16)
    copies[total].wait()
    live = live_rows(count[0, 0], queries.shape[0])
    live_out[...] = live
    copies[1].wait()
    grad_rows = (cot[...].astype(jnp.float32) * live).astype(jnp.bfloat16)
    copies[4].wait()
    grad_out[...] = mm(grad_rows, w_out[...], NT).astype(jnp.bfloat16)
    for copy in copies[5:total]:
        copy.wait()


def join(own, partner, out):
    out[: own.shape[0], :] = own[...]
    out[own.shape[0] :, :] = partner[...]


def attention(ops, kind, heads, grads, gain, w_key, w_value, *refs):
    total = len(ops)
    blocks, (own_out, send_out, keep_out, mixed_out, dq_out) = refs[:-5], refs[-5:]
    own, partner, across, got, other = blocks[0], blocks[1], blocks[2], blocks[3 : 3 + total], blocks[3 + total]
    size = own.shape[0]
    pair = 2 * size
    branch = lax.axis_index("branch")
    core, volume = branch % 2, (branch >= lax.axis_size("branch") // 2).astype(jnp.int32)

    def ordered(first, second):
        return jnp.where(core == 0, first, second), jnp.where(core == 0, second, first)

    sides = ([own[...], partner[...]], [across[...], other[:size, :]])
    for k, (_, _, near, far) in enumerate(ops):
        at = size + k * pair
        here, there = got[k][...], other[at : at + pair, :]
        if near != far:
            here, there = ordered(here, there)
        sides[near].append(here)
        sides[far].append(there)
    anchors = jnp.concatenate(sides[0] + sides[1], 0)
    half = anchors.shape[0] // 2
    center, scale = centered(anchors)
    normed = (center * scale * as_row(gain)).astype(jnp.bfloat16)
    keys = mm(normed, w_key[...], NN).astype(jnp.bfloat16)
    values = mm(normed, w_value[...], NN).astype(jnp.bfloat16)

    width = keys.shape[1]
    head = width // HEADS
    rows = heads.shape[0]
    score_scale = 1.0 / head**0.5
    lanes = 2 * head
    first = lax.broadcasted_iota(jnp.int32, (1, lanes), 1) < head
    zero = jnp.zeros((), jnp.bfloat16)
    is_near = (kind[...] == 1).astype(jnp.int32) == volume
    is_near = jnp.concatenate([is_near.astype(jnp.int32)] * 2, 1) == 1

    def stack(x):
        return jnp.concatenate([jnp.where(first, x, zero), jnp.where(first, zero, x)], 0)

    def unstack(x):
        return jnp.where(first, x[:rows], x[rows:]).astype(jnp.bfloat16)

    def pick(x):
        return jnp.where(is_near, x[:half], x[half:])

    def spread(x):
        x = x.astype(jnp.float32)
        return jnp.concatenate(
            [jnp.where(is_near, x, 0.0), jnp.where(is_near, 0.0, x)], 0
        ).astype(jnp.bfloat16)

    key_grads, value_grads = [], []
    for at in range(0, width, lanes):
        span = slice(at, at + lanes)
        key, value = keys[:, span], values[:, span]
        query, grad = stack(heads[:, span]), stack(grads[:, span])
        scores = pick(mm(key, query, NT)) * score_scale
        expo = jnp.exp(scores - jnp.max(scores, axis=0, keepdims=True))
        probs = expo / jnp.sum(expo, axis=0, keepdims=True)
        probs_all = spread(probs)
        grad_probs = pick(mm(value, grad, NT))
        delta = jnp.sum(grad_probs * probs, axis=0, keepdims=True)
        grad_scores = spread(probs * (grad_probs - delta) * score_scale)
        mixed_out[:, span] = unstack(mm(probs_all, value, TN))
        dq_out[:, span] = unstack(mm(grad_scores, key, TN))
        key_grads.append(mm(grad_scores, query, NN))
        value_grads.append(mm(probs_all, grad, NN))
    projected = None
    for parts, weight in ((key_grads, w_key), (value_grads, w_value)):
        whole = jnp.concatenate(parts, 1)
        high = whole.astype(jnp.bfloat16)
        low = (whole - high.astype(jnp.float32)).astype(jnp.bfloat16)
        term = mm(high, weight[...], NT) + mm(low, weight[...], NT)
        projected = term if projected is None else projected + term

    own_out[...] = projected[:size]
    send_out[:size, :] = projected[size:pair].astype(jnp.bfloat16)
    keep_out[:size, :] = projected[half : half + size]
    send_out[size:pair, :] = projected[half + size : half + pair].astype(jnp.bfloat16)
    starts = [pair, half + pair]

    def take(side):
        at = starts[side]
        starts[side] = at + pair
        return projected[at : at + pair]

    for k, (_, _, near, far) in enumerate(ops):
        here, there = take(near), take(far)
        if near != far:
            here, there = ordered(here, there)
        keep_out[size + k * pair : size + (k + 1) * pair, :] = here
        send_out[pair + k * pair : pair + (k + 1) * pair, :] = there.astype(jnp.bfloat16)


def query_back(live, queries, cot, mixed, dq, gain, w_query, w_out, fields, query_grad):
    residual = queries[...].astype(jnp.float32) + mm(mixed[...], w_out[...], NN)
    fields[...] = (live[...] * residual).astype(jnp.bfloat16)
    center, scale = centered(queries[...])
    back = norm_pullback(center, scale, as_row(gain), mm(dq[...], w_query[...], NT))
    query_grad[...] = live[...] * (cot[...].astype(jnp.float32) + back)


def add_partner(own, keep, got, own_out, across, *sums):
    size = own.shape[0]
    pair = 2 * size
    own_out[...] = own[...] + got[:size, :].astype(jnp.float32)
    across[...] = (keep[:size, :] + got[size:pair, :].astype(jnp.float32)).astype(across.dtype)
    for k, out in enumerate(sums):
        at = size + k * pair
        kept = keep[at : at + pair, :]
        out[...] = (kept + got[size + at : size + at + pair, :].astype(jnp.float32)).astype(out.dtype)


def add_chips(*refs):
    got, (own, own_out, send_out) = refs[:-3], refs[-3:]
    size = own.shape[0]
    total = got[0][...].astype(jnp.float32)
    for other in got[1:]:
        total = total + other[...].astype(jnp.float32)
    own_out[...] = own[...] + total[:size]
    send_out[...] = total[size:].astype(send_out.dtype)


def anchor_back(anchors, own, got, across, gain, out):
    center, scale = centered(anchors[...])
    grad = own[...] + got[...].astype(jnp.float32) + across[...].astype(jnp.float32)
    out[...] = norm_pullback(center, scale, as_row(gain), grad)


def call(body, outs, *args, staged=()):
    specs = [pl.BlockSpec(memory_space=pltpu.VMEM)] * len(args)
    placed = [pltpu.with_memory_space_constraint(x, pltpu.VMEM) for x in args]
    held = [x if x.size == 1 else pltpu.with_memory_space_constraint(x, pltpu.HBM) for x in staged]
    return pl.pallas_call(
        body,
        out_shape=[pltpu.VMEM(*out) if on_chip else jax.ShapeDtypeStruct(*out) for on_chip, *out in outs],
        in_specs=specs + [pl.BlockSpec(memory_space=pl.ANY if x.size == 1 else pltpu.HBM) for x in staged],
        out_specs=[pl.BlockSpec(memory_space=pltpu.VMEM)] * len(outs),
        scratch_shapes=[pltpu.SMEM((1, 1), jnp.int32), pltpu.SemaphoreType.DMA((len(held),))] if held else [],
        compiler_params=pltpu.CompilerParams(vmem_limit_bytes=32 * 2**20),
    )(*placed, *held)


def exchange_plan(branches, pts):
    near_bit, top = pts, branches * pts // 2
    nears = [d for d in range(1, top) if not d & near_bit]
    plan = [(d, d | top) for d in reversed(nears)]
    return [(a, b, int(a >= top), int(b >= top)) for a, b in plan]


def on_device(sizes, anchors, queries, query_kind, live_count, anchor_gain, query_gain, w_query, w_key, w_value, w_out, cotangent):
    branches, pts = sizes
    group = branches * pts
    plan = exchange_plan(branches, pts)

    def send(x, deltas):
        return lax.ppermute(x, GROUP_AXES, [(i, i ^ deltas[(i // pts) % 2]) for i in range(group)])

    def swap(x):
        return send(x, (pts, pts))

    def cross(x):
        return send(x, (group // 2, group // 2))

    size, width = anchors.shape
    rows = queries.shape[0]
    pair = 2 * size
    f32, bf16 = jnp.float32, jnp.bfloat16
    partner = swap(anchors)
    across = cross(anchors)
    (chip,) = call(join, [(True, (pair, width), bf16)], anchors, partner)
    got = []
    for step in plan:
        got.append(send(chip, step))
    inputs = (queries, cotangent, query_gain, w_query, w_out, anchors, anchor_gain, w_key, w_value, query_kind.reshape(1, -1))
    (heads, grads, live, queries, cotangent, query_gain, w_query, w_out, anchors, anchor_gain, w_key, w_value, query_kind) = call(
        query_side,
        [(True, (rows, width), bf16)] * 2 + [(True, (rows, 1), f32)] + [(True, x.shape, x.dtype) for x in inputs],
        staged=inputs + (live_count.reshape(1, 1),),
    )
    other = swap(jnp.concatenate([across] + got, 0))
    own, outgoing, keep, mixed, dq = call(
        functools.partial(attention, plan),
        [
            (True, (size, width), f32),
            (True, (pair + pair * len(plan), width), bf16),
            (True, (size + pair * len(plan), width), f32),
            (True, (rows, width), bf16),
            (True, (rows, width), bf16),
        ],
        query_kind,
        heads,
        grads,
        anchor_gain,
        w_key,
        w_value,
        anchors,
        partner,
        across,
        *got,
        other,
    )
    fields, query_grad = call(
        query_back, [(False, (rows, width), bf16), (False, (rows, width), f32)],
        live, queries, cotangent, mixed, dq, query_gain, w_query, w_out,
    )
    incoming = swap(outgoing)
    own, across, *sums = call(
        add_partner,
        [(True, (size, width), f32), (True, (size, width), bf16)] + [(True, (pair, width), bf16)] * len(plan),
        own,
        keep,
        incoming,
    )
    arrived = []
    for part, step in zip(sums, plan):
        arrived.append(send(part, step))
    across = cross(across)
    own, last = call(add_chips, [(True, (size, width), f32), (True, (size, width), bf16)], *arrived, own)
    last = swap(last)
    (anchor_grad,) = call(anchor_back, [(False, (size, width), f32)], anchors, own, last, across, anchor_gain)
    return fields, query_grad, anchor_grad


def solution(mesh):
    split = P(("car",) + GROUP_AXES, None)
    flat = P(("car",) + GROUP_AXES)
    sizes = mesh.shape["branch"], mesh.shape["pts"]

    def body(*args):
        return on_device(sizes, *args)

    return jax.shard_map(
        body,
        mesh=mesh,
        in_specs=(split, split, flat, flat, P(), P(), P(), P(), P(), P(), split),
        out_specs=(split, split, split),
        check_vma=False,
    )
```

profile of v0, /device:TPU:0, one launch (start us, length us, event | category | flops | bytes accessed | tf_op | source)
XLA Modules:
  0.0 30.5 jit_solution(6142092857703888501)
XLA Ops:
  0.6 0.6 %collective-permute-start = (bf16[16,384]{1,0:T(8,128)(2,1)}, bf16[16,384]{1,0:T(8,128)(2,1)S(1)}, u32[]{:S(2)}, u32[]{:S(2)}) collective-permute-start(bf16[16,384]{1,0:T(8,128)(2,1)} %own.1), channel_id=1, source_target_pairs={{0,4},{1,5},{2,6},{3,7},{4,0},{5,1},{6,2},{7,3},{8,12},{9,13},{10,... | collective-permute-start | bytes 36872 | tf_op jit(solution)/shard_map/ppermute | solution.py:232
  1.2 1.0 %collective-permute-done.partner.refs_1_ = bf16[16,384]{1,0:T(8,128)(2,1)S(1)} collective-permute-done((bf16[16,384]{1,0:T(8,128)(2,1)}, bf16[16,384]{1,0:T(8,128)(2,1)S(1)}, u32[]{:S(2)}, u32[]{:S(2)}) %collective-permute-start) | collective-permute-done | bytes 12320 | tf_op jit(solution)/shard_map/ppermute | solution.py:232
  2.2 0.0 copy-start
  2.2 0.7 %copy-done = bf16[16,384]{1,0:T(8,128)(2,1)S(1)} copy-done((bf16[16,384]{1,0:T(8,128)(2,1)S(1)}, bf16[16,384]{1,0:T(8,128)(2,1)}, u32[]{:S(2)}) %copy-start) | copy-done | bytes 12312
  2.9 2.9 %collective-permute-start.4 = (bf16[32,384]{1,0:T(8,128)(2,1)S(1)}, bf16[32,384]{1,0:T(8,128)(2,1)S(1)}, u32[]{:S(2)}, u32[]{:S(2)}) collective-permute-start(bf16[32,384]{1,0:T(8,128)(2,1)S(1)} %shard_map.131), channel_id=1, source_target_pairs={{0,1},{1,0},{2,3},{3,2},{4,13},{5,12},{6,15},{7,14},{8,9},{9,8},{1... | collective-permute-start | bytes 73736 | tf_op jit(solution)/shard_map/ppermute | solution.py:232
  5.8 2.6 %collective-permute-start.3 = (bf16[32,384]{1,0:T(8,128)(2,1)S(1)}, bf16[32,384]{1,0:T(8,128)(2,1)S(1)}, u32[]{:S(2)}, u32[]{:S(2)}) collective-permute-start(bf16[32,384]{1,0:T(8,128)(2,1)S(1)} %shard_map.131), channel_id=1, source_target_pairs={{0,2},{1,3},{2,0},{3,1},{4,14},{5,15},{6,12},{7,13},{8,10},{9,11},... | collective-permute-start | bytes 73736 | tf_op jit(solution)/shard_map/ppermute | solution.py:232
  8.4 0.0 collective-permute-start.2
  8.4 1.7 %collective-permute-start.1 = (bf16[16,384]{1,0:T(8,128)(2,1)S(1)}, bf16[16,384]{1,0:T(8,128)(2,1)S(1)}, u32[]{:S(2)}, u32[]{:S(2)}) collective-permute-start(bf16[16,384]{1,0:T(8,128)(2,1)S(1)} %copy-done), channel_id=1, source_target_pairs={{0,8},{1,9},{2,10},{3,11},{4,12},{5,13},{6,14},{7,15},{8,0},{9,1},... | collective-permute-start | bytes 36872 | tf_op jit(solution)/shard_map/ppermute | solution.py:232
  10.2 2.0 %collective-permute-done.1.refs_2_ = bf16[16,384]{1,0:T(8,128)(2,1)S(1)} collective-permute-done((bf16[16,384]{1,0:T(8,128)(2,1)S(1)}, bf16[16,384]{1,0:T(8,128)(2,1)S(1)}, u32[]{:S(2)}, u32[]{:S(2)}) %collective-permute-start.1) | collective-permute-done | bytes 12320 | tf_op jit(solution)/shard_map/ppermute | solution.py:232
  12.1 0.0 collective-permute-done.4.refs_5_
  12.1 0.0 collective-permute-done.3.refs_4_
  12.1 1.9 %collective-permute-done.2.refs_3_ = bf16[32,384]{1,0:T(8,128)(2,1)S(1)} collective-permute-done((bf16[32,384]{1,0:T(8,128)(2,1)S(1)}, bf16[32,384]{1,0:T(8,128)(2,1)S(1)}, u32[]{:S(2)}, u32[]{:S(2)}) %collective-permute-start.2) | collective-permute-done | bytes 24608 | tf_op jit(solution)/shard_map/ppermute | solution.py:232
  14.1 0.3 %collective-permute-start.5 = (bf16[112,384]{1,0:T(8,128)(2,1)S(1)}, bf16[112,384]{1,0:T(8,128)(2,1)S(1)}, u32[]{:S(2)}, u32[]{:S(2)}) collective-permute-start(bf16[112,384]{1,0:T(8,128)(2,1)S(1)} %pad_maximum_fusion), channel_id=1, source_target_pairs={{0,4},{1,5},{2,6},{3,7},{4,0},{5,1},{6,2},{7,3},{8,12},{9,13},{10,... | collective-permute-start | bytes 258056 | tf_op jit(solution)/shard_map/ppermute | solution.py:232
  15.0 1.7 %shard_map.130 = (bf16[128,384]{1,0:T(8,128)(2,1)S(1)}, bf16[128,384]{1,0:T(8,128)(2,1)S(1)}, f32[128,1]{1,0:T(8,128)S(1)}, bf16[128,384]{1,0:T(8,128)(2,1)S(1)}...) custom-call(bf16[128,384]{1,0:T(8,128)(2,1)} %refs_0_.1, ...), custom_call_target="tpu_custom_call" | custom-call | tf_op jit(solution)/shard_map/pallas_call | solution.py:209
  16.8 0.0 collective-permute-done.5.refs_6_
  16.8 2.4 %shard_map.132 = (f32[16,384]{1,0:T(8,128)S(1)}, bf16[128,384]{1,0:T(8,128)(2,1)S(1)}, f32[112,384]{1,0:T(8,128)S(1)}, bf16[128,384]{1,0:T(8,128)(2,1)S(1)}, bf16[128,384]{1,0:T(8,128)(2,1)S(1)}) custom-call(s32[1,128]{1,0:T(1,128)S(1)} %get-tuple-element.33.kind, bf16[128,384]{1,0:T(8,128)(2,1)S(1)} %get-tuple-element.34.heads, ...), custom_call_target="tpu_custom_call" | custom-call | tf_op jit(solution)/shard_map/pallas_call | solution.py:209
  19.2 0.3 %collective-permute-start.6 = (bf16[128,384]{1,0:T(8,128)(2,1)S(1)}, bf16[128,384]{1,0:T(8,128)(2,1)S(1)}, u32[]{:S(2)}, u32[]{:S(2)}) collective-permute-start(bf16[128,384]{1,0:T(8,128)(2,1)S(1)} %get-tuple-element.49), channel_id=1, source_target_pairs={{0,4},{1,5},{2,6},{3,7},{4,0},{5,1},{6,2},{7,3},{8,12},{9,13},{10,... | collective-permute-start | bytes 294920 | tf_op jit(solution)/shard_map/ppermute | solution.py:232
  19.6 1.0 %collective-permute-done.6.got = bf16[128,384]{1,0:T(8,128)(2,1)S(1)} collective-permute-done((bf16[128,384]{1,0:T(8,128)(2,1)S(1)}, bf16[128,384]{1,0:T(8,128)(2,1)S(1)}, u32[]{:S(2)}, u32[]{:S(2)}) %collective-permute-start.6) | collective-permute-done | bytes 98336 | tf_op jit(solution)/shard_map/ppermute | solution.py:232
  20.6 1.9 %collective-permute-start.7 = (bf16[32,384]{1,0:T(8,128)(2,1)S(1)}, bf16[32,384]{1,0:T(8,128)(2,1)S(1)}, u32[]{:S(2)}, u32[]{:S(2)}) collective-permute-start(bf16[32,384]{1,0:T(8,128)(2,1)S(1)} %get-tuple-element.50), channel_id=1, source_target_pairs={{0,3},{1,2},{2,1},{3,0},{4,15},{5,14},{6,13},{7,12},{8,11},{9,10},... | collective-permute-start | bytes 73736 | tf_op jit(solution)/shard_map/ppermute | solution.py:232
  22.5 0.0 collective-permute-start.8
  22.5 2.5 %collective-permute-start.9 = (bf16[32,384]{1,0:T(8,128)(2,1)S(1)}, bf16[32,384]{1,0:T(8,128)(2,1)S(1)}, u32[]{:S(2)}, u32[]{:S(2)}) collective-permute-start(bf16[32,384]{1,0:T(8,128)(2,1)S(1)} %get-tuple-element.52), channel_id=1, source_target_pairs={{0,1},{1,0},{2,3},{3,2},{4,13},{5,12},{6,15},{7,14},{8,9},{9,8},{1... | collective-permute-start | bytes 73736 | tf_op jit(solution)/shard_map/ppermute | solution.py:232
  25.1 1.5 %collective-permute-start.11 = (bf16[16,384]{1,0:T(8,128)(2,1)S(1)}, bf16[16,384]{1,0:T(8,128)(2,1)S(1)}, u32[]{:S(2)}, u32[]{:S(2)}) collective-permute-start(bf16[16,384]{1,0:T(8,128)(2,1)S(1)} %get-tuple-element.56), channel_id=1, source_target_pairs={{0,8},{1,9},{2,10},{3,11},{4,12},{5,13},{6,14},{7,15},{8,0},{9,1},... | collective-permute-start | bytes 36872 | tf_op jit(solution)/shard_map/ppermute | solution.py:232
  26.6 0.0 collective-permute-done.7.refs_0_
  26.6 1.1 %collective-permute-done.8.refs_1_ = bf16[32,384]{1,0:T(8,128)(2,1)S(1)} collective-permute-done((bf16[32,384]{1,0:T(8,128)(2,1)S(1)}, bf16[32,384]{1,0:T(8,128)(2,1)S(1)}, u32[]{:S(2)}, u32[]{:S(2)}) %collective-permute-start.8) | collective-permute-done | bytes 24608 | tf_op jit(solution)/shard_map/ppermute | solution.py:232
  27.7 0.0 collective-permute-done.9.refs_2_
  27.7 0.7 %collective-permute-start.10 = (bf16[16,384]{1,0:T(8,128)(2,1)S(1)}, bf16[16,384]{1,0:T(8,128)(2,1)S(1)}, u32[]{:S(2)}, u32[]{:S(2)}) collective-permute-start(bf16[16,384]{1,0:T(8,128)(2,1)S(1)} %get-tuple-element.55), channel_id=1, source_target_pairs={{0,4},{1,5},{2,6},{3,7},{4,0},{5,1},{6,2},{7,3},{8,12},{9,13},{10,... | collective-permute-start | bytes 36872 | tf_op jit(solution)/shard_map/ppermute | solution.py:232
  28.4 1.2 %shard_map.133 = (bf16[128,384]{1,0:T(8,128)(2,1)}, f32[128,384]{1,0:T(8,128)}) custom-call(f32[128,1]{1,0:T(8,128)S(1)} %get-tuple-element.30.live, bf16[128,384]{1,0:T(8,128)(2,1)S(1)} %get-tuple-element.31.queries, bf16[128,384]{1,0:T(8,128)(2,1)S(1)} %get-tuple-element.32.cot, bf16[128,384]{1,0:T(8,128)(2,1)S(1)} %get-tuple-element.40.mixed, ...), custom_call_target="tpu_custom_call" | custom-call | tf_op jit(solution)/shard_map/pallas_call | solution.py:209
  29.6 0.0 collective-permute-done.11.across
  29.6 0.0 collective-permute-done.10.got
  29.6 0.9 %shard_map.136 = f32[16,384]{1,0:T(8,128)} custom-call(bf16[16,384]{1,0:T(8,128)(2,1)S(1)} %get-tuple-element.39.refs_0_.anchors, f32[16,384]{1,0:T(8,128)S(1)} %get-tuple-element.54.own, bf16[16,384]{1,0:T(8,128)(2,1)S(1)} %collective-permute-done.10.got, bf16[16,384]{1,0:T(8,128)(2,1)S(1)} %collective-permute-done.11.across, f32[384]{0:T(512)S(1)} %get-tuple-element.36.gain), custom_call_target="tpu_custom_call" | custom-call | tf_op jit(solution)/shard_map/pallas_call | solution.py:209
  (4 shorter events, 0.1 us)
Async XLA Ops:
  0.6 1.6 %collective-permute-start = (bf16[16,384]{1,0:T(8,128)(2,1)}, bf16[16,384]{1,0:T(8,128)(2,1)S(1)}, u32[]{:S(2)}, u32[]{:S(2)}) collective-permute-start(bf16[16,384]{1,0:T(8,128)(2,1)} %own.1), channel_id=1, source_target_pairs={{0,4},{1,5},{2,6},{3,7},{4,0},{5,1},{6,2},{7,3},{8,12},{9,13},{10,... | collective-permute-start | bytes 36872 | tf_op jit(solution)/shard_map/ppermute | solution.py:232
  2.2 0.7 %copy-start = (bf16[16,384]{1,0:T(8,128)(2,1)S(1)}, bf16[16,384]{1,0:T(8,128)(2,1)}, u32[]{:S(2)}) copy-start(bf16[16,384]{1,0:T(8,128)(2,1)} %own.1) | copy-start | bytes 36868
  2.9 9.2 %collective-permute-start.4 = (bf16[32,384]{1,0:T(8,128)(2,1)S(1)}, bf16[32,384]{1,0:T(8,128)(2,1)S(1)}, u32[]{:S(2)}, u32[]{:S(2)}) collective-permute-start(bf16[32,384]{1,0:T(8,128)(2,1)S(1)} %shard_map.131), channel_id=1, source_target_pairs={{0,1},{1,0},{2,3},{3,2},{4,13},{5,12},{6,15},{7,14},{8,9},{9,8},{1... | collective-permute-start | bytes 73736 | tf_op jit(solution)/shard_map/ppermute | solution.py:232
  5.8 6.3 %collective-permute-start.3 = (bf16[32,384]{1,0:T(8,128)(2,1)S(1)}, bf16[32,384]{1,0:T(8,128)(2,1)S(1)}, u32[]{:S(2)}, u32[]{:S(2)}) collective-permute-start(bf16[32,384]{1,0:T(8,128)(2,1)S(1)} %shard_map.131), channel_id=1, source_target_pairs={{0,2},{1,3},{2,0},{3,1},{4,14},{5,15},{6,12},{7,13},{8,10},{9,11},... | collective-permute-start | bytes 73736 | tf_op jit(solution)/shard_map/ppermute | solution.py:232
  8.4 5.6 %collective-permute-start.2 = (bf16[32,384]{1,0:T(8,128)(2,1)S(1)}, bf16[32,384]{1,0:T(8,128)(2,1)S(1)}, u32[]{:S(2)}, u32[]{:S(2)}) collective-permute-start(bf16[32,384]{1,0:T(8,128)(2,1)S(1)} %shard_map.131), channel_id=1, source_target_pairs={{0,3},{1,2},{2,1},{3,0},{4,15},{5,14},{6,13},{7,12},{8,11},{9,10},... | collective-permute-start | bytes 73736 | tf_op jit(solution)/shard_map/ppermute | solution.py:232
  8.4 3.7 %collective-permute-start.1 = (bf16[16,384]{1,0:T(8,128)(2,1)S(1)}, bf16[16,384]{1,0:T(8,128)(2,1)S(1)}, u32[]{:S(2)}, u32[]{:S(2)}) collective-permute-start(bf16[16,384]{1,0:T(8,128)(2,1)S(1)} %copy-done), channel_id=1, source_target_pairs={{0,8},{1,9},{2,10},{3,11},{4,12},{5,13},{6,14},{7,15},{8,0},{9,1},... | collective-permute-start | bytes 36872 | tf_op jit(solution)/shard_map/ppermute | solution.py:232
  14.1 2.7 %collective-permute-start.5 = (bf16[112,384]{1,0:T(8,128)(2,1)S(1)}, bf16[112,384]{1,0:T(8,128)(2,1)S(1)}, u32[]{:S(2)}, u32[]{:S(2)}) collective-permute-start(bf16[112,384]{1,0:T(8,128)(2,1)S(1)} %pad_maximum_fusion), channel_id=1, source_target_pairs={{0,4},{1,5},{2,6},{3,7},{4,0},{5,1},{6,2},{7,3},{8,12},{9,13},{10,... | collective-permute-start | bytes 258056 | tf_op jit(solution)/shard_map/ppermute | solution.py:232
  19.2 1.4 %collective-permute-start.6 = (bf16[128,384]{1,0:T(8,128)(2,1)S(1)}, bf16[128,384]{1,0:T(8,128)(2,1)S(1)}, u32[]{:S(2)}, u32[]{:S(2)}) collective-permute-start(bf16[128,384]{1,0:T(8,128)(2,1)S(1)} %get-tuple-element.49), channel_id=1, source_target_pairs={{0,4},{1,5},{2,6},{3,7},{4,0},{5,1},{6,2},{7,3},{8,12},{9,13},{10,... | collective-permute-start | bytes 294920 | tf_op jit(solution)/shard_map/ppermute | solution.py:232
  20.6 6.0 %collective-permute-start.7 = (bf16[32,384]{1,0:T(8,128)(2,1)S(1)}, bf16[32,384]{1,0:T(8,128)(2,1)S(1)}, u32[]{:S(2)}, u32[]{:S(2)}) collective-permute-start(bf16[32,384]{1,0:T(8,128)(2,1)S(1)} %get-tuple-element.50), channel_id=1, source_target_pairs={{0,3},{1,2},{2,1},{3,0},{4,15},{5,14},{6,13},{7,12},{8,11},{9,10},... | collective-permute-start | bytes 73736 | tf_op jit(solution)/shard_map/ppermute | solution.py:232
  22.5 5.2 %collective-permute-start.8 = (bf16[32,384]{1,0:T(8,128)(2,1)S(1)}, bf16[32,384]{1,0:T(8,128)(2,1)S(1)}, u32[]{:S(2)}, u32[]{:S(2)}) collective-permute-start(bf16[32,384]{1,0:T(8,128)(2,1)S(1)} %get-tuple-element.51), channel_id=1, source_target_pairs={{0,2},{1,3},{2,0},{3,1},{4,14},{5,15},{6,12},{7,13},{8,10},{9,11},... | collective-permute-start | bytes 73736 | tf_op jit(solution)/shard_map/ppermute | solution.py:232
  22.5 5.2 %collective-permute-start.9 = (bf16[32,384]{1,0:T(8,128)(2,1)S(1)}, bf16[32,384]{1,0:T(8,128)(2,1)S(1)}, u32[]{:S(2)}, u32[]{:S(2)}) collective-permute-start(bf16[32,384]{1,0:T(8,128)(2,1)S(1)} %get-tuple-element.52), channel_id=1, source_target_pairs={{0,1},{1,0},{2,3},{3,2},{4,13},{5,12},{6,15},{7,14},{8,9},{9,8},{1... | collective-permute-start | bytes 73736 | tf_op jit(solution)/shard_map/ppermute | solution.py:232
  25.1 4.5 %collective-permute-start.11 = (bf16[16,384]{1,0:T(8,128)(2,1)S(1)}, bf16[16,384]{1,0:T(8,128)(2,1)S(1)}, u32[]{:S(2)}, u32[]{:S(2)}) collective-permute-start(bf16[16,384]{1,0:T(8,128)(2,1)S(1)} %get-tuple-element.56), channel_id=1, source_target_pairs={{0,8},{1,9},{2,10},{3,11},{4,12},{5,13},{6,14},{7,15},{8,0},{9,1},... | collective-permute-start | bytes 36872 | tf_op jit(solution)/shard_map/ppermute | solution.py:232
  27.7 1.9 %collective-permute-start.10 = (bf16[16,384]{1,0:T(8,128)(2,1)S(1)}, bf16[16,384]{1,0:T(8,128)(2,1)S(1)}, u32[]{:S(2)}, u32[]{:S(2)}) collective-permute-start(bf16[16,384]{1,0:T(8,128)(2,1)S(1)} %get-tuple-element.55), channel_id=1, source_target_pairs={{0,4},{1,5},{2,6},{3,7},{4,0},{5,1},{6,2},{7,3},{8,12},{9,13},{10,... | collective-permute-start | bytes 36872 | tf_op jit(solution)/shard_map/ppermute | solution.py:232
where the time goes:
time: 30.7 us; the launch traced here: 30.5 us
  starting transfers between devices  15.1 us (49%)
  waiting for transfers between devices  7.11 us (23%)
  Pallas kernels  6.27 us (20%)
  between operations  1.33 us (4%)
  local copies, waits for them, and re-layouts  0.71 us (2%)
    ppermute x12, starting transfers between devices, send(): lax.ppermute(x, GROUP_AXES, [(i, i ^ deltas[i // pts % 2]) for i in range...  15.1 us
    ppermute x12, waiting for transfers between devices, send(): lax.ppermute(x, GROUP_AXES, [(i, i ^ deltas[i // pts % 2]) for i in range...  7.11 us
    pallas_call x7, Pallas kernels, call(): pl.pallas_call(body, out_shape=[pltpu.VMEM(*out) if on_chip else jax.Shap...  6.27 us
    unnamed x2, local copies, waits for them, and re-layouts  0.71 us
  transfers between devices with their start and end apart: 12, of which 5 were waited for; matrix products, arithmetic and copies ran while one was open for 0% of the time, Pallas kernels for 10%

commit v1 on v0

v1 whole, which is shorter than its diff:
```python
import functools

import jax
import jax.numpy as jnp
from jax import lax
from jax.experimental import pallas as pl
from jax.experimental.pallas import tpu as pltpu
from jax.sharding import PartitionSpec as P


HEADS = 6
GROUP_AXES = ("branch", "pts")

NN = (((1,), (0,)), ((), ()))
NT = (((1,), (1,)), ((), ()))
TN = (((0,), (0,)), ((), ()))


def mm(a, b, dims):
    return lax.dot_general(a, b, dims, preferred_element_type=jnp.float32)


def centered(rows):
    values = rows.astype(jnp.float32)
    center = values - jnp.mean(values, axis=-1, keepdims=True)
    variance = jnp.mean(center * center, axis=-1, keepdims=True)
    return center, lax.rsqrt(variance + 1e-05)


def norm_pullback(center, scale, gain, grad):
    through = grad * gain
    inner = jnp.mean(through * center, axis=-1, keepdims=True)
    grad_center = scale * through - center * (scale * scale * scale * inner)
    return grad_center - jnp.mean(grad_center, axis=-1, keepdims=True)


def as_row(gain):
    return gain[...].reshape(1, -1)


def live_rows(count, rows):
    return (lax.broadcasted_iota(jnp.int32, (rows, 1), 0) < count).astype(jnp.float32)


def masked_pair(pair, head):
    first = lax.broadcasted_iota(jnp.int32, (1, 2 * head), 1) < head
    zero = jnp.zeros((), pair.dtype)
    return jnp.concatenate([jnp.where(first, pair, zero), jnp.where(first, zero, pair)], 0)


def put_pairs(out, rows, head):
    height = 2 * rows.shape[0]
    for k in range(rows.shape[1] // (2 * head)):
        out[k * height : (k + 1) * height, :] = masked_pair(rows[:, 2 * head * k : 2 * head * (k + 1)], head)


def query_side(queries, cot, gain, w_query, w_out, *refs):
    total = (len(refs) - 6) // 2
    sources, outs, count, sems = refs[: total + 1], refs[total + 1 : -2], refs[-2], refs[-1]
    (heads_out, grad_out, live_out), kept = outs[:3], outs[3:]
    copies = [pltpu.make_async_copy(a, b, sems.at[k]) for k, (a, b) in enumerate(zip(sources, kept + (count,)))]
    for copy in copies:
        copy.start()
    center, scale = centered(queries[...])
    query_normed = (center * scale * as_row(gain)).astype(jnp.bfloat16)
    width = queries.shape[1]
    heads = mm(query_normed, w_query[...], NN).astype(jnp.bfloat16)
    put_pairs(heads_out, heads * (1.0 / (width // HEADS) ** 0.5), width // HEADS)
    copies[total].wait()
    live = live_rows(count[0, 0], queries.shape[0])
    live_out[...] = live
    grad_rows = (cot[...].astype(jnp.float32) * live).astype(jnp.bfloat16)
    put_pairs(grad_out, mm(grad_rows, w_out[...], NT).astype(jnp.bfloat16), width // HEADS)
    for copy in copies[:total]:
        copy.wait()


def stage(*refs):
    total = len(refs) // 2
    copies = [pltpu.make_async_copy(refs[k], refs[total + k], refs[-1].at[k]) for k in range(total)]
    for copy in copies:
        copy.start()
    for copy in copies:
        copy.wait()


def join(own, partner, out):
    out[: own.shape[0], :] = own[...]
    out[own.shape[0] :, :] = partner[...]


def where_am_i():
    branch = lax.axis_index("branch")
    return branch % 2, (branch >= lax.axis_size("branch") // 2).astype(jnp.int32)


def ordered(first, second):
    core, _ = where_am_i()
    return jnp.where(core == 0, first, second), jnp.where(core == 0, second, first)


def attend(near, anchors, kind, heads, grads, gain, w_key, w_value, mixed_out, dq_out):
    center, scale = centered(anchors)
    normed = (center * scale * as_row(gain)).astype(jnp.bfloat16)
    keys = mm(normed, w_key[...], NN).astype(jnp.bfloat16)
    values = mm(normed, w_value[...], NN).astype(jnp.bfloat16)
    width = keys.shape[1]
    head = width // HEADS
    rows = kind.shape[1]
    score_scale = 1.0 / head**0.5
    _, volume = where_am_i()
    mine = (kind[...] == 1).astype(jnp.int32) == (volume if near else 1 - volume)
    mine = jnp.concatenate([mine.astype(jnp.int32)] * 2, 1) == 1

    def by_head(x):
        return jnp.concatenate([x[:, :rows], x[:, rows:]], 0)

    key_grads, value_grads = [], []

    def span(k):
        return slice(2 * head * k, 2 * head * (k + 1))

    def lines(k):
        return slice(2 * rows * k, 2 * rows * (k + 1))

    def products(k):
        return mm(keys[:, span(k)], heads[lines(k), :], NT), mm(values[:, span(k)], grads[lines(k), :], NT)

    def soften(scores, grad_probs):
        expo = jnp.exp(scores - jnp.max(scores, axis=0, keepdims=True))
        total = jnp.sum(expo, axis=0, keepdims=True)
        probs = expo * jnp.where(mine, 1.0 / total, 0.0)
        delta = jnp.sum(grad_probs * probs, axis=0, keepdims=True)
        return probs.astype(jnp.bfloat16), (probs * (grad_probs - delta)).astype(jnp.bfloat16)

    def outputs(k, probs, grad_scores):
        key_grads.append(mm(grad_scores, heads[lines(k), :], NN).astype(jnp.bfloat16))
        value_grads.append(mm(probs, grads[lines(k), :], NN).astype(jnp.bfloat16))
        mixed = mm(by_head(probs), masked_pair(values[:, span(k)], head), TN)
        mixed_out[:, span(k)] = mixed.astype(jnp.bfloat16)
        dq = mm(by_head(grad_scores), masked_pair(keys[:, span(k)], head), TN)
        dq_out[:, span(k)] = (dq * score_scale).astype(jnp.bfloat16)

    pairs = width // (2 * head)
    raw = [products(k) for k in range(pairs)]
    soft = [soften(*x) for x in raw]
    for k in range(pairs):
        outputs(k, *soft[k])
    key_grad, value_grad = jnp.concatenate(key_grads, 1), jnp.concatenate(value_grads, 1)
    return mm(key_grad, w_key[...], NT) + mm(value_grad, w_value[...], NT)


def near_side(counts, kind, heads, grads, gain, w_key, w_value, own, partner, *refs):
    both, split, _ = counts
    (got, other), (own_out, send_out, keep_out, mixed_out, dq_out) = refs[:2], refs[2:]
    size = own.shape[0]
    pair = 2 * size
    blocks = [own[...], partner[...], got[: both * pair, :], other[: both * pair, :]]
    for k in range(both, both + split):
        at = slice(k * pair, (k + 1) * pair)
        blocks.append(ordered(got[at, :], other[at, :])[0])
    grad = attend(True, jnp.concatenate(blocks, 0), kind, heads, grads, gain, w_key, w_value, mixed_out, dq_out)
    middle = pair + both * pair
    own_out[...] = grad[:size]
    send_out[:size, :] = grad[size:pair].astype(jnp.bfloat16)
    send_out[size:, :] = grad[middle : middle + both * pair].astype(jnp.bfloat16)
    keep_out[: both * pair, :] = grad[pair:middle]
    keep_out[both * pair :, :] = grad[middle + both * pair :]


def far_side(counts, kind, heads, grads, gain, w_key, w_value, got, other, got_far, other_far, kept, *refs):
    both, split, far = counts
    send_out, keep_out, mixed_out, dq_out = refs
    pair = got.shape[0] // (both + split)
    size = pair // 2
    span = far * pair + size
    blocks = [got_far[...], other_far[...]]
    for k in range(both, both + split):
        at = slice(k * pair, (k + 1) * pair)
        blocks.append(ordered(got[at, :], other[at, :])[1])
    grad = attend(False, jnp.concatenate(blocks, 0), kind, heads, grads, gain, w_key, w_value, mixed_out, dq_out)
    keep_out[:span, :] = grad[:span]
    send_out[:span, :] = grad[span : 2 * span].astype(jnp.bfloat16)
    here, there = ordered(kept[both * pair :, :], grad[2 * span :])
    keep_out[span:, :] = here
    send_out[span:, :] = there.astype(jnp.bfloat16)


def field_rows(live, queries, near, far, w_out, fields):
    residual = queries[...].astype(jnp.float32) + mm(near[...] + far[...], w_out[...], NN)
    fields[...] = (live[...] * residual).astype(jnp.bfloat16)


def query_back(live, queries, cot, near, far, gain, w_query, query_grad):
    center, scale = centered(queries[...])
    back = norm_pullback(center, scale, as_row(gain), mm(near[...] + far[...], w_query[...], NT))
    query_grad[...] = live[...] * (cot[...].astype(jnp.float32) + back)


def add_near(own, keep, got, own_out, *sums):
    size = own.shape[0]
    pair = 2 * size
    own_out[...] = own[...] + got[:size, :].astype(jnp.float32)
    for k, out in enumerate(sums):
        at = k * pair
        out[...] = (keep[at : at + pair, :] + got[size + at : size + at + pair, :].astype(jnp.float32)).astype(out.dtype)


def add_far(keep, got, *sums):
    at = 0
    for out in sums:
        span = slice(at, at + out.shape[0])
        out[...] = (keep[span, :] + got[span, :].astype(jnp.float32)).astype(out.dtype)
        at += out.shape[0]


def add_chips(*refs):
    got, (own, own_out, send_out) = refs[:-3], refs[-3:]
    size = own.shape[0]
    total = got[0][...].astype(jnp.float32)
    for other in got[1:]:
        total = total + other[...].astype(jnp.float32)
    own_out[...] = own[...] + total[:size]
    send_out[...] = total[size:].astype(send_out.dtype)


def anchor_back(anchors, own, got, across, gain, out):
    center, scale = centered(anchors[...])
    grad = own[...] + got[...].astype(jnp.float32) + across[...].astype(jnp.float32)
    out[...] = norm_pullback(center, scale, as_row(gain), grad)


def call(body, outs, *args, staged=(), scratch=()):
    specs = [pl.BlockSpec(memory_space=pltpu.VMEM)] * len(args)
    placed = [pltpu.with_memory_space_constraint(x, pltpu.VMEM) for x in args]
    held = [x if x.size == 1 else pltpu.with_memory_space_constraint(x, pltpu.HBM) for x in staged]
    return pl.pallas_call(
        body,
        out_shape=[pltpu.VMEM(*out) if on_chip else jax.ShapeDtypeStruct(*out) for on_chip, *out in outs],
        in_specs=specs + [pl.BlockSpec(memory_space=pl.ANY if x.size == 1 else pltpu.HBM) for x in staged],
        out_specs=[pl.BlockSpec(memory_space=pltpu.VMEM)] * len(outs),
        scratch_shapes=list(scratch),
        compiler_params=pltpu.CompilerParams(vmem_limit_bytes=32 * 2**20),
    )(*placed, *held)


def exchange_plan(branches, pts):
    top = branches * pts // 2
    nears = [d for d in range(1, top) if not d & pts]
    fars = [d | top for d in nears]
    both = list(zip(nears[:-1:2], nears[1:-1:2]))
    far = list(zip(fars[:-1:2], fars[1:-1:2]))
    return both + [(nears[-1], fars[-1])] + far, (len(both), 1, len(far))


def on_device(sizes, anchors, queries, query_kind, live_count, anchor_gain, query_gain, w_query, w_key, w_value, w_out, cotangent):
    branches, pts = sizes
    group = branches * pts
    plan, counts = exchange_plan(branches, pts)
    both, split, far = counts
    early = both + split

    def send(x, deltas):
        return lax.ppermute(x, GROUP_AXES, [(i, i ^ deltas[(i // pts) % 2]) for i in range(group)])

    def swap(x):
        return send(x, (pts, pts))

    def cross(x):
        return send(x, (group // 2, group // 2))

    size, width = anchors.shape
    rows = queries.shape[0]
    pair = 2 * size
    f32, bf16 = jnp.float32, jnp.bfloat16
    stacked = (HEADS * rows, 2 * width // HEADS)
    partner = swap(anchors)
    needed = (anchors, queries, cotangent, query_gain, w_query, w_out)
    local, queries, cotangent, query_gain, w_query, w_out = call(
        stage,
        [(True, x.shape, x.dtype) for x in needed],
        staged=needed,
        scratch=[pltpu.SemaphoreType.DMA((len(needed),))],
    )
    (chip,) = call(join, [(True, (pair, width), bf16)], local, partner)
    got = []
    for step in plan:
        got.append(send(chip, step))
    across = cross(anchors)
    inputs = (anchor_gain, w_key, w_value, query_kind.reshape(1, -1))
    heads, grads, live, anchor_gain, w_key, w_value, query_kind = call(
        query_side,
        [(True, stacked, bf16)] * 2 + [(True, (rows, 1), f32)] + [(True, x.shape, x.dtype) for x in inputs],
        queries,
        cotangent,
        query_gain,
        w_query,
        w_out,
        staged=inputs + (live_count.reshape(1, 1),),
        scratch=[pltpu.SMEM((1, 1), jnp.int32), pltpu.SemaphoreType.DMA((len(inputs) + 1,))],
    )
    got_near = jnp.concatenate(got[:early], 0)
    other_near = swap(got_near)
    got_far = jnp.concatenate([across] + got[early:], 0)
    other_far = swap(got_far)
    common = (query_kind, heads, grads, anchor_gain, w_key, w_value)
    rowwise = [(True, (rows, width), bf16)] * 2
    own, send_near, keep_near, mixed_near, dq_near = call(
        functools.partial(near_side, counts),
        [(True, (size, width), f32), (True, (size + pair * both, width), bf16), (True, (pair * early, width), f32)] + rowwise,
        *common,
        local,
        partner,
        got_near,
        other_near,
    )
    back_near = swap(send_near)
    send_far, keep_far, mixed_far, dq_far = call(
        functools.partial(far_side, counts),
        [(True, (size + pair * (far + split), width), bf16), (True, (size + pair * (far + split), width), f32)] + rowwise,
        *common,
        got_near,
        other_near,
        got_far,
        other_far,
        keep_near,
    )
    back_far = swap(send_far)
    own, *sums = call(
        add_near, [(True, (size, width), f32)] + [(True, (pair, width), bf16)] * both, own, keep_near, back_near
    )
    across, *more = call(
        add_far, [(True, (size, width), bf16)] + [(True, (pair, width), bf16)] * (far + split), keep_far, back_far
    )
    sums += more[far:] + more[:far]
    arrived = []
    for part, step in zip(sums, plan):
        arrived.append(send(part, step))
    across = cross(across)
    (fields,) = call(field_rows, [(False, (rows, width), bf16)], live, queries, mixed_near, mixed_far, w_out)
    (query_grad,) = call(
        query_back, [(False, (rows, width), f32)],
        live, queries, cotangent, dq_near, dq_far, query_gain, w_query,
    )
    own, last = call(add_chips, [(True, (size, width), f32), (True, (size, width), bf16)], *arrived, own)
    last = swap(last)
    (anchor_grad,) = call(anchor_back, [(False, (size, width), f32)], local, own, last, across, anchor_gain)
    return fields, query_grad, anchor_grad


def solution(mesh):
    split = P(("car",) + GROUP_AXES, None)
    flat = P(("car",) + GROUP_AXES)
    sizes = mesh.shape["branch"], mesh.shape["pts"]

    def body(*args):
        return on_device(sizes, *args)

    return jax.shard_map(
        body,
        mesh=mesh,
        in_specs=(split, split, flat, flat, P(), P(), P(), P(), P(), P(), split),
        out_specs=(split, split, split),
        check_vma=False,
    )
```

time: 30.7 us -> 31.1 us (1.013)
  Pallas kernels: 6.27 us -> 7.69 us
  local copies, waits for them, and re-layouts: 0.71 us -> 0.02 us
    pallas_call x7 -> x11, Pallas kernels: 6.27 us -> 7.69 us  [call(): pl.pallas_call(body, out_shape=[pltpu.VMEM(*out) if on_chip else jax.Shap...]
    unnamed x2, local copies, waits for them, and re-layouts: 0.71 us -> 0.01 us
    ppermute x12 -> x14, starting transfers between devices: 15.1 us -> 14.8 us  [send(): lax.ppermute(x, GROUP_AXES, [(i, i ^ deltas[i // pts % 2]) for i in range...]
    ppermute x12 -> x14, waiting for transfers between devices: 7.11 us -> 7.05 us  [send(): lax.ppermute(x, GROUP_AXES, [(i, i ^ deltas[i // pts % 2]) for i in range...]
  transfers between devices with their start and end apart: 12 -> 14, of which waited for: 5 -> 4; matrix products, arithmetic and copies ran while one was open for 0% -> 0% of each run, Pallas kernels for 10% -> 18%
where the time goes in v1:
time: 31.1 us; the launch traced here: 30.9 us
  starting transfers between devices  14.8 us (48%)
  Pallas kernels  7.69 us (25%)
  waiting for transfers between devices  7.05 us (23%)
  between operations  1.37 us (4%)
    ppermute x14, starting transfers between devices, send(): lax.ppermute(x, GROUP_AXES, [(i, i ^ deltas[i // pts % 2]) for i in range...  14.8 us
    pallas_call x11, Pallas kernels, call(): pl.pallas_call(body, out_shape=[pltpu.VMEM(*out) if on_chip else jax.Shap...  7.69 us
    ppermute x14, waiting for transfers between devices, send(): lax.ppermute(x, GROUP_AXES, [(i, i ^ deltas[i // pts % 2]) for i in range...  7.05 us
  transfers between devices with their start and end apart: 14, of which 4 were waited for; matrix products, arithmetic and copies ran while one was open for 0% of the time, Pallas kernels for 18%

profile of v1, /device:TPU:0, one launch (start us, length us, event | category | flops | bytes accessed | tf_op | source)
XLA Modules:
  0.0 30.9 jit_solution(15952792693856540000)
XLA Ops:
  0.6 0.6 %collective-permute-start = (bf16[16,384]{1,0:T(8,128)(2,1)}, bf16[16,384]{1,0:T(8,128)(2,1)S(1)}, u32[]{:S(2)}, u32[]{:S(2)}) collective-permute-start(bf16[16,384]{1,0:T(8,128)(2,1)} %refs_0_.2), channel_id=1, source_target_pairs={{0,4},{1,5},{2,6},{3,7},{4,0},{5,1},{6,2},{7,3},{8,12},{9,13},{10,... | collective-permute-start | bytes 36872 | tf_op jit(solution)/shard_map/ppermute | solution.py:264
  1.2 2.6 %collective-permute-start.4 = (bf16[16,384]{1,0:T(8,128)(2,1)}, bf16[16,384]{1,0:T(8,128)(2,1)S(1)}, u32[]{:S(2)}, u32[]{:S(2)}) collective-permute-start(bf16[16,384]{1,0:T(8,128)(2,1)} %refs_0_.2), channel_id=1, source_target_pairs={{0,8},{1,9},{2,10},{3,11},{4,12},{5,13},{6,14},{7,15},{8,0},{9,1},... | collective-permute-start | bytes 36872 | tf_op jit(solution)/shard_map/ppermute | solution.py:264
  3.7 1.2 %shard_map.130 = (bf16[16,384]{1,0:T(8,128)(2,1)S(1)}, bf16[128,384]{1,0:T(8,128)(2,1)S(1)}, bf16[128,384]{1,0:T(8,128)(2,1)S(1)}, f32[384]{0:T(512)S(1)}, bf16[...) custom-call(bf16[16,384]{1,0:T(8,128)(2,1)} %refs_0_.2, bf16[128,384]{1,0:T(8,128)(2,1)} %refs_1_.2, ...), custom_call_target="tpu_custom_call" | custom-call | tf_op jit(solution)/shard_map/pallas_call | solution.py:237
  5.0 0.0 collective-permute-done.partner
  5.0 1.6 %collective-permute-start.5 = (bf16[32,384]{1,0:T(8,128)(2,1)S(1)}, bf16[32,384]{1,0:T(8,128)(2,1)S(1)}, u32[]{:S(2)}, u32[]{:S(2)}) collective-permute-start(bf16[32,384]{1,0:T(8,128)(2,1)S(1)} %shard_map.132), channel_id=1, source_target_pairs={{0,9},{1,8},{2,11},{3,10},{4,14},{5,15},{6,12},{7,13},{8,1},{9,0},... | collective-permute-start | bytes 73736 | tf_op jit(solution)/shard_map/ppermute | solution.py:264
  6.6 2.5 %collective-permute-start.2 = (bf16[32,384]{1,0:T(8,128)(2,1)S(1)}, bf16[32,384]{1,0:T(8,128)(2,1)S(1)}, u32[]{:S(2)}, u32[]{:S(2)}) collective-permute-start(bf16[32,384]{1,0:T(8,128)(2,1)S(1)} %shard_map.132), channel_id=1, source_target_pairs={{0,3},{1,2},{2,1},{3,0},{4,15},{5,14},{6,13},{7,12},{8,11},{9,10},... | collective-permute-start | bytes 73736 | tf_op jit(solution)/shard_map/ppermute | solution.py:264
  9.1 0.7 %collective-permute-start.1 = (bf16[32,384]{1,0:T(8,128)(2,1)S(1)}, bf16[32,384]{1,0:T(8,128)(2,1)S(1)}, u32[]{:S(2)}, u32[]{:S(2)}) collective-permute-start(bf16[32,384]{1,0:T(8,128)(2,1)S(1)} %shard_map.132), channel_id=1, source_target_pairs={{0,1},{1,0},{2,3},{3,2},{4,6},{5,7},{6,4},{7,5},{8,9},{9,8},{10,11... | collective-permute-start | bytes 73736 | tf_op jit(solution)/shard_map/ppermute | solution.py:264
  9.8 0.0 collective-permute-done.4
  9.8 3.2 %collective-permute-done.1 = bf16[32,384]{1,0:T(8,128)(2,1)S(1)} collective-permute-done((bf16[32,384]{1,0:T(8,128)(2,1)S(1)}, bf16[32,384]{1,0:T(8,128)(2,1)S(1)}, u32[]{:S(2)}, u32[]{:S(2)}) %collective-permute-start.1) | collective-permute-done | bytes 24608 | tf_op jit(solution)/shard_map/ppermute | solution.py:264
  12.9 0.6 %collective-permute-start.3 = (bf16[64,384]{1,0:T(8,128)(2,1)S(1)}, bf16[64,384]{1,0:T(8,128)(2,1)S(1)}, u32[]{:S(2)}, u32[]{:S(2)}) collective-permute-start(bf16[64,384]{1,0:T(8,128)(2,1)S(1)} %constant_dynamic-update-slice_fusion.refs_0_.got), channel_id=1, source_target_pairs={{0,4},{1,5},{2,6},{3,7},{4,0},{5,1},{6,2},{7,3},{8,12},{9,13},{10,... | collective-permute-start | bytes 147464 | tf_op jit(solution)/shard_map/ppermute | solution.py:264
  13.5 0.0 collective-permute-done.5
  13.5 0.1 collective-permute-start.6
  14.3 1.3 %shard_map.131 = (bf16[768,128]{1,0:T(8,128)(2,1)S(1)}, bf16[768,128]{1,0:T(8,128)(2,1)S(1)}, f32[128,1]{1,0:T(8,128)S(1)}, f32[384]{0:T(512)S(1)}, bf16[384,384...) custom-call(bf16[128,384]{1,0:T(8,128)(2,1)S(1)} %get-tuple-element.32.queries, ...), custom_call_target="tpu_custom_call" | custom-call | tf_op jit(solution)/shard_map/pallas_call | solution.py:237
  15.5 0.0 collective-permute-done.3.refs_1_.other
  15.6 1.2 %shard_map.133 = (f32[16,384]{1,0:T(8,128)S(1)}, bf16[48,384]{1,0:T(8,128)(2,1)S(1)}, f32[64,384]{1,0:T(8,128)S(1)}, bf16[128,384]{1,0:T(8,128)(2,1)S(1)}, bf16[128,384]{1,0:T(8,128)(2,1)S(1)}) custom-call(s32[1,128]{1,0:T(1,128)S(1)} %get-tuple-element.38.kind, bf16[768,128]{1,0:T(8,128)(2,1)S(1)} %get-tuple-element.39.heads, ...), custom_call_target="tpu_custom_call" | custom-call | tf_op jit(solution)/shard_map/pallas_call | solution.py:237
  16.7 1.2 %shard_map.134 = (bf16[80,384]{1,0:T(8,128)(2,1)S(1)}, f32[80,384]{1,0:T(8,128)S(1)}, bf16[128,384]{1,0:T(8,128)(2,1)S(1)}, bf16[128,384]{1,0:T(8,128)(2,1)S(1)}) custom-call(s32[1,128]{1,0:T(1,128)S(1)} %get-tuple-element.38.kind, bf16[768,128]{1,0:T(8,128)(2,1)S(1)} %get-tuple-element.39.heads, bf16[768,128]{1,0:T(8,128)(2,1)S(1)} %get-tuple-element.40.grads, ...), custom_call_target="tpu_custom_call" | custom-call | tf_op jit(solution)/shard_map/pallas_call | solution.py:237
  17.9 0.6 %collective-permute-start.9 = (bf16[80,384]{1,0:T(8,128)(2,1)S(1)}, bf16[80,384]{1,0:T(8,128)(2,1)S(1)}, u32[]{:S(2)}, u32[]{:S(2)}) collective-permute-start(bf16[80,384]{1,0:T(8,128)(2,1)S(1)} %get-tuple-element.54), channel_id=1, source_target_pairs={{0,4},{1,5},{2,6},{3,7},{4,0},{5,1},{6,2},{7,3},{8,12},{9,13},{10,... | collective-permute-start | bytes 184328 | tf_op jit(solution)/shard_map/ppermute | solution.py:264
  18.5 0.1 collective-permute-start.7
  18.5 1.1 %collective-permute-done.7.got = bf16[48,384]{1,0:T(8,128)(2,1)S(1)} collective-permute-done((bf16[48,384]{1,0:T(8,128)(2,1)S(1)}, bf16[48,384]{1,0:T(8,128)(2,1)S(1)}, u32[]{:S(2)}, u32[]{:S(2)}) %collective-permute-start.7) | collective-permute-done | bytes 36896 | tf_op jit(solution)/shard_map/ppermute | solution.py:264
  19.7 0.4 %collective-permute-start.8 = (bf16[32,384]{1,0:T(8,128)(2,1)S(1)}, bf16[32,384]{1,0:T(8,128)(2,1)S(1)}, u32[]{:S(2)}, u32[]{:S(2)}) collective-permute-start(bf16[32,384]{1,0:T(8,128)(2,1)S(1)} %get-tuple-element.52), channel_id=1, source_target_pairs={{0,1},{1,0},{2,3},{3,2},{4,6},{5,7},{6,4},{7,5},{8,9},{9,8},{10,11... | collective-permute-start | bytes 73736 | tf_op jit(solution)/shard_map/ppermute | solution.py:264
  20.1 0.0 collective-permute-done.9.got
  20.1 2.6 %collective-permute-start.10 = (bf16[32,384]{1,0:T(8,128)(2,1)S(1)}, bf16[32,384]{1,0:T(8,128)(2,1)S(1)}, u32[]{:S(2)}, u32[]{:S(2)}) collective-permute-start(bf16[32,384]{1,0:T(8,128)(2,1)S(1)} %get-tuple-element.55), channel_id=1, source_target_pairs={{0,3},{1,2},{2,1},{3,0},{4,15},{5,14},{6,13},{7,12},{8,11},{9,10},... | collective-permute-start | bytes 73736 | tf_op jit(solution)/shard_map/ppermute | solution.py:264
  22.7 0.8 %collective-permute-start.11 = (bf16[32,384]{1,0:T(8,128)(2,1)S(1)}, bf16[32,384]{1,0:T(8,128)(2,1)S(1)}, u32[]{:S(2)}, u32[]{:S(2)}) collective-permute-start(bf16[32,384]{1,0:T(8,128)(2,1)S(1)} %get-tuple-element.56), channel_id=1, source_target_pairs={{0,9},{1,8},{2,11},{3,10},{4,14},{5,15},{6,12},{7,13},{8,1},{9,0},... | collective-permute-start | bytes 73736 | tf_op jit(solution)/shard_map/ppermute | solution.py:264
  23.5 1.3 %collective-permute-start.13 = (bf16[16,384]{1,0:T(8,128)(2,1)S(1)}, bf16[16,384]{1,0:T(8,128)(2,1)S(1)}, u32[]{:S(2)}, u32[]{:S(2)}) collective-permute-start(bf16[16,384]{1,0:T(8,128)(2,1)S(1)} %get-tuple-element.60), channel_id=1, source_target_pairs={{0,8},{1,9},{2,10},{3,11},{4,12},{5,13},{6,14},{7,15},{8,0},{9,1},... | collective-permute-start | bytes 36872 | tf_op jit(solution)/shard_map/ppermute | solution.py:264
  24.8 0.0 collective-permute-done.8.refs_0_
  24.8 1.2 %collective-permute-done.10.refs_1_ = bf16[32,384]{1,0:T(8,128)(2,1)S(1)} collective-permute-done((bf16[32,384]{1,0:T(8,128)(2,1)S(1)}, bf16[32,384]{1,0:T(8,128)(2,1)S(1)}, u32[]{:S(2)}, u32[]{:S(2)}) %collective-permute-start.10) | collective-permute-done | bytes 24608 | tf_op jit(solution)/shard_map/ppermute | solution.py:264
  26.0 1.5 %collective-permute-done.11.refs_2_ = bf16[32,384]{1,0:T(8,128)(2,1)S(1)} collective-permute-done((bf16[32,384]{1,0:T(8,128)(2,1)S(1)}, bf16[32,384]{1,0:T(8,128)(2,1)S(1)}, u32[]{:S(2)}, u32[]{:S(2)}) %collective-permute-start.11) | collective-permute-done | bytes 24608 | tf_op jit(solution)/shard_map/ppermute | solution.py:264
  27.6 0.5 %collective-permute-start.12 = (bf16[16,384]{1,0:T(8,128)(2,1)S(1)}, bf16[16,384]{1,0:T(8,128)(2,1)S(1)}, u32[]{:S(2)}, u32[]{:S(2)}) collective-permute-start(bf16[16,384]{1,0:T(8,128)(2,1)S(1)} %get-tuple-element.59), channel_id=1, source_target_pairs={{0,4},{1,5},{2,6},{3,7},{4,0},{5,1},{6,2},{7,3},{8,12},{9,13},{10,... | collective-permute-start | bytes 36872 | tf_op jit(solution)/shard_map/ppermute | solution.py:264
  28.1 1.1 %shard_map.136 = f32[128,384]{1,0:T(8,128)} custom-call(f32[128,1]{1,0:T(8,128)S(1)} %get-tuple-element.37.live, bf16[128,384]{1,0:T(8,128)(2,1)S(1)} %get-tuple-element.32.queries, bf16[128,384]{1,0:T(8,128)(2,1)S(1)} %get-tuple-element.33.cot, bf16[128,384]{1,0:T(8,128)(2,1)S(1)} %get-tuple-element.48.near, bf16[128,384]{1,0:T(8,128)(2,1)S(1)} %get-tuple-element.49.far, ...), custom_call_target="tpu_custom_call" | custom-call | tf_op jit(solution)/shard_map/pallas_call | solution.py:237
  29.2 0.9 %shard_map.135 = bf16[128,384]{1,0:T(8,128)(2,1)} custom-call(f32[128,1]{1,0:T(8,128)S(1)} %get-tuple-element.37.live, bf16[128,384]{1,0:T(8,128)(2,1)S(1)} %get-tuple-element.32.queries, bf16[128,384]{1,0:T(8,128)(2,1)S(1)} %get-tuple-element.45.near, bf16[128,384]{1,0:T(8,128)(2,1)S(1)} %get-tuple-element.47.far, bf16[384,384]{1,0:T(8,128)(2,1)S(1)} %get-tuple-element.36.w_out), custom_call_target="tpu_custom_call" | custom-call | tf_op jit(solution)/shard_map/pallas_call | solution.py:237
  30.0 0.0 collective-permute-done.12.got
  30.0 0.9 %shard_map.140 = f32[16,384]{1,0:T(8,128)} custom-call(bf16[16,384]{1,0:T(8,128)(2,1)S(1)} %get-tuple-element.44.own.anchors, f32[16,384]{1,0:T(8,128)S(1)} %get-tuple-element.58.own, bf16[16,384]{1,0:T(8,128)(2,1)S(1)} %collective-permute-done.12.got, bf16[16,384]{1,0:T(8,128)(2,1)S(1)} %collective-permute-done.13.across, f32[384]{0:T(512)S(1)} %get-tuple-element.41.gain), custom_call_target="tpu_custom_call" | custom-call | tf_op jit(solution)/shard_map/pallas_call | solution.py:237
  (11 shorter events, 0.1 us)
Async XLA Ops:
  0.6 4.4 %collective-permute-start = (bf16[16,384]{1,0:T(8,128)(2,1)}, bf16[16,384]{1,0:T(8,128)(2,1)S(1)}, u32[]{:S(2)}, u32[]{:S(2)}) collective-permute-start(bf16[16,384]{1,0:T(8,128)(2,1)} %refs_0_.2), channel_id=1, source_target_pairs={{0,4},{1,5},{2,6},{3,7},{4,0},{5,1},{6,2},{7,3},{8,12},{9,13},{10,... | collective-permute-start | bytes 36872 | tf_op jit(solution)/shard_map/ppermute | solution.py:264
  1.2 8.6 %collective-permute-start.4 = (bf16[16,384]{1,0:T(8,128)(2,1)}, bf16[16,384]{1,0:T(8,128)(2,1)S(1)}, u32[]{:S(2)}, u32[]{:S(2)}) collective-permute-start(bf16[16,384]{1,0:T(8,128)(2,1)} %refs_0_.2), channel_id=1, source_target_pairs={{0,8},{1,9},{2,10},{3,11},{4,12},{5,13},{6,14},{7,15},{8,0},{9,1},... | collective-permute-start | bytes 36872 | tf_op jit(solution)/shard_map/ppermute | solution.py:264
  5.0 8.5 %collective-permute-start.5 = (bf16[32,384]{1,0:T(8,128)(2,1)S(1)}, bf16[32,384]{1,0:T(8,128)(2,1)S(1)}, u32[]{:S(2)}, u32[]{:S(2)}) collective-permute-start(bf16[32,384]{1,0:T(8,128)(2,1)S(1)} %shard_map.132), channel_id=1, source_target_pairs={{0,9},{1,8},{2,11},{3,10},{4,14},{5,15},{6,12},{7,13},{8,1},{9,0},... | collective-permute-start | bytes 73736 | tf_op jit(solution)/shard_map/ppermute | solution.py:264
  6.6 6.3 %collective-permute-start.2 = (bf16[32,384]{1,0:T(8,128)(2,1)S(1)}, bf16[32,384]{1,0:T(8,128)(2,1)S(1)}, u32[]{:S(2)}, u32[]{:S(2)}) collective-permute-start(bf16[32,384]{1,0:T(8,128)(2,1)S(1)} %shard_map.132), channel_id=1, source_target_pairs={{0,3},{1,2},{2,1},{3,0},{4,15},{5,14},{6,13},{7,12},{8,11},{9,10},... | collective-permute-start | bytes 73736 | tf_op jit(solution)/shard_map/ppermute | solution.py:264
  9.1 3.8 %collective-permute-start.1 = (bf16[32,384]{1,0:T(8,128)(2,1)S(1)}, bf16[32,384]{1,0:T(8,128)(2,1)S(1)}, u32[]{:S(2)}, u32[]{:S(2)}) collective-permute-start(bf16[32,384]{1,0:T(8,128)(2,1)S(1)} %shard_map.132), channel_id=1, source_target_pairs={{0,1},{1,0},{2,3},{3,2},{4,6},{5,7},{6,4},{7,5},{8,9},{9,8},{10,11... | collective-permute-start | bytes 73736 | tf_op jit(solution)/shard_map/ppermute | solution.py:264
  12.9 2.6 %collective-permute-start.3 = (bf16[64,384]{1,0:T(8,128)(2,1)S(1)}, bf16[64,384]{1,0:T(8,128)(2,1)S(1)}, u32[]{:S(2)}, u32[]{:S(2)}) collective-permute-start(bf16[64,384]{1,0:T(8,128)(2,1)S(1)} %constant_dynamic-update-slice_fusion.refs_0_.got), channel_id=1, source_target_pairs={{0,4},{1,5},{2,6},{3,7},{4,0},{5,1},{6,2},{7,3},{8,12},{9,13},{10,... | collective-permute-start | bytes 147464 | tf_op jit(solution)/shard_map/ppermute | solution.py:264
  13.5 3.2 %collective-permute-start.6 = (bf16[48,384]{1,0:T(8,128)(2,1)S(1)}, bf16[48,384]{1,0:T(8,128)(2,1)S(1)}, u32[]{:S(2)}, u32[]{:S(2)}) collective-permute-start(bf16[48,384]{1,0:T(8,128)(2,1)S(1)} %constant_dynamic-update-slice_fusion.2.got_far), channel_id=1, source_target_pairs={{0,4},{1,5},{2,6},{3,7},{4,0},{5,1},{6,2},{7,3},{8,12},{9,13},{10,... | collective-permute-start | bytes 110600 | tf_op jit(solution)/shard_map/ppermute | solution.py:264
  17.9 2.2 %collective-permute-start.9 = (bf16[80,384]{1,0:T(8,128)(2,1)S(1)}, bf16[80,384]{1,0:T(8,128)(2,1)S(1)}, u32[]{:S(2)}, u32[]{:S(2)}) collective-permute-start(bf16[80,384]{1,0:T(8,128)(2,1)S(1)} %get-tuple-element.54), channel_id=1, source_target_pairs={{0,4},{1,5},{2,6},{3,7},{4,0},{5,1},{6,2},{7,3},{8,12},{9,13},{10,... | collective-permute-start | bytes 184328 | tf_op jit(solution)/shard_map/ppermute | solution.py:264
  18.5 1.2 %collective-permute-start.7 = (bf16[48,384]{1,0:T(8,128)(2,1)S(1)}, bf16[48,384]{1,0:T(8,128)(2,1)S(1)}, u32[]{:S(2)}, u32[]{:S(2)}) collective-permute-start(bf16[48,384]{1,0:T(8,128)(2,1)S(1)} %get-tuple-element.51), channel_id=1, source_target_pairs={{0,4},{1,5},{2,6},{3,7},{4,0},{5,1},{6,2},{7,3},{8,12},{9,13},{10,... | collective-permute-start | bytes 110600 | tf_op jit(solution)/shard_map/ppermute | solution.py:264
  19.7 5.1 %collective-permute-start.8 = (bf16[32,384]{1,0:T(8,128)(2,1)S(1)}, bf16[32,384]{1,0:T(8,128)(2,1)S(1)}, u32[]{:S(2)}, u32[]{:S(2)}) collective-permute-start(bf16[32,384]{1,0:T(8,128)(2,1)S(1)} %get-tuple-element.52), channel_id=1, source_target_pairs={{0,1},{1,0},{2,3},{3,2},{4,6},{5,7},{6,4},{7,5},{8,9},{9,8},{10,11... | collective-permute-start | bytes 73736 | tf_op jit(solution)/shard_map/ppermute | solution.py:264
  20.1 5.9 %collective-permute-start.10 = (bf16[32,384]{1,0:T(8,128)(2,1)S(1)}, bf16[32,384]{1,0:T(8,128)(2,1)S(1)}, u32[]{:S(2)}, u32[]{:S(2)}) collective-permute-start(bf16[32,384]{1,0:T(8,128)(2,1)S(1)} %get-tuple-element.55), channel_id=1, source_target_pairs={{0,3},{1,2},{2,1},{3,0},{4,15},{5,14},{6,13},{7,12},{8,11},{9,10},... | collective-permute-start | bytes 73736 | tf_op jit(solution)/shard_map/ppermute | solution.py:264
  22.7 4.8 %collective-permute-start.11 = (bf16[32,384]{1,0:T(8,128)(2,1)S(1)}, bf16[32,384]{1,0:T(8,128)(2,1)S(1)}, u32[]{:S(2)}, u32[]{:S(2)}) collective-permute-start(bf16[32,384]{1,0:T(8,128)(2,1)S(1)} %get-tuple-element.56), channel_id=1, source_target_pairs={{0,9},{1,8},{2,11},{3,10},{4,14},{5,15},{6,12},{7,13},{8,1},{9,0},... | collective-permute-start | bytes 73736 | tf_op jit(solution)/shard_map/ppermute | solution.py:264
  23.5 6.5 %collective-permute-start.13 = (bf16[16,384]{1,0:T(8,128)(2,1)S(1)}, bf16[16,384]{1,0:T(8,128)(2,1)S(1)}, u32[]{:S(2)}, u32[]{:S(2)}) collective-permute-start(bf16[16,384]{1,0:T(8,128)(2,1)S(1)} %get-tuple-element.60), channel_id=1, source_target_pairs={{0,8},{1,9},{2,10},{3,11},{4,12},{5,13},{6,14},{7,15},{8,0},{9,1},... | collective-permute-start | bytes 36872 | tf_op jit(solution)/shard_map/ppermute | solution.py:264
  27.6 2.5 %collective-permute-start.12 = (bf16[16,384]{1,0:T(8,128)(2,1)S(1)}, bf16[16,384]{1,0:T(8,128)(2,1)S(1)}, u32[]{:S(2)}, u32[]{:S(2)}) collective-permute-start(bf16[16,384]{1,0:T(8,128)(2,1)S(1)} %get-tuple-element.59), channel_id=1, source_target_pairs={{0,4},{1,5},{2,6},{3,7},{4,0},{5,1},{6,2},{7,3},{8,12},{9,13},{10,... | collective-permute-start | bytes 36872 | tf_op jit(solution)/shard_map/ppermute | solution.py:264

commit v2 on v1

--- a/solution.py
+++ b/solution.py
@@ -84,6 +84,13 @@
         copy.wait()
 
 
+def pack(*refs):
+    at = 0
+    for ref in refs[:-1]:
+        refs[-1][at : at + ref.shape[0], :] = ref[...]
+        at += ref.shape[0]
+
+
 def join(own, partner, out):
     out[: own.shape[0], :] = own[...]
     out[own.shape[0] :, :] = partner[...]
@@ -299,7 +306,7 @@
         staged=inputs + (live_count.reshape(1, 1),),
         scratch=[pltpu.SMEM((1, 1), jnp.int32), pltpu.SemaphoreType.DMA((len(inputs) + 1,))],
     )
-    got_near = jnp.concatenate(got[:early], 0)
+    (got_near,) = call(pack, [(True, (pair * early, width), bf16)], *got[:early])
     other_near = swap(got_near)
     got_far = jnp.concatenate([across] + got[early:], 0)
     other_far = swap(got_far)

time: 31.1 us -> 31 us (level)
    pallas_call x11 -> x12, Pallas kernels: 7.69 us -> 7.7 us  [call(): pl.pallas_call(body, out_shape=[pltpu.VMEM(*out) if on_chip else jax.Shap...]
  transfers between devices with their start and end apart: 14 -> 14, of which waited for: 4 -> 5; matrix products, arithmetic and copies ran while one was open for 0% -> 0% of each run, Pallas kernels for 18% -> 18%
where the time goes in v2:
time: 31 us; the launch traced here: 30.8 us
  starting transfers between devices  14.7 us (47%)
  Pallas kernels  7.7 us (25%)
  waiting for transfers between devices  7.05 us (23%)
  between operations  1.37 us (4%)
    ppermute x14, starting transfers between devices, send(): lax.ppermute(x, GROUP_AXES, [(i, i ^ deltas[i // pts % 2]) for i in range...  14.7 us
    pallas_call x12, Pallas kernels, call(): pl.pallas_call(body, out_shape=[pltpu.VMEM(*out) if on_chip else jax.Shap...  7.7 us
    ppermute x14, waiting for transfers between devices, send(): lax.ppermute(x, GROUP_AXES, [(i, i ^ deltas[i // pts % 2]) for i in range...  7.05 us
  transfers between devices with their start and end apart: 14, of which 5 were waited for; matrix products, arithmetic and copies ran while one was open for 0% of the time, Pallas kernels for 18%

profile of v2, /device:TPU:0, one launch (start us, length us, event | category | flops | bytes accessed | tf_op | source)
XLA Modules:
  0.0 30.8 jit_solution(7335986612414812782)
XLA Ops:
  0.6 0.6 %collective-permute-start = (bf16[16,384]{1,0:T(8,128)(2,1)}, bf16[16,384]{1,0:T(8,128)(2,1)S(1)}, u32[]{:S(2)}, u32[]{:S(2)}) collective-permute-start(bf16[16,384]{1,0:T(8,128)(2,1)} %refs_0_.2), channel_id=1, source_target_pairs={{0,4},{1,5},{2,6},{3,7},{4,0},{5,1},{6,2},{7,3},{8,12},{9,13},{10,... | collective-permute-start | bytes 36872 | tf_op jit(solution)/shard_map/ppermute | solution.py:271
  1.2 2.6 %collective-permute-start.4 = (bf16[16,384]{1,0:T(8,128)(2,1)}, bf16[16,384]{1,0:T(8,128)(2,1)S(1)}, u32[]{:S(2)}, u32[]{:S(2)}) collective-permute-start(bf16[16,384]{1,0:T(8,128)(2,1)} %refs_0_.2), channel_id=1, source_target_pairs={{0,8},{1,9},{2,10},{3,11},{4,12},{5,13},{6,14},{7,15},{8,0},{9,1},... | collective-permute-start | bytes 36872 | tf_op jit(solution)/shard_map/ppermute | solution.py:271
  3.7 1.2 %shard_map.130 = (bf16[16,384]{1,0:T(8,128)(2,1)S(1)}, bf16[128,384]{1,0:T(8,128)(2,1)S(1)}, bf16[128,384]{1,0:T(8,128)(2,1)S(1)}, f32[384]{0:T(512)S(1)}, bf16[...) custom-call(bf16[16,384]{1,0:T(8,128)(2,1)} %refs_0_.2, bf16[128,384]{1,0:T(8,128)(2,1)} %refs_1_.2, ...), custom_call_target="tpu_custom_call" | custom-call | tf_op jit(solution)/shard_map/pallas_call | solution.py:244
  5.0 0.0 collective-permute-done.partner
  5.0 1.6 %collective-permute-start.5 = (bf16[32,384]{1,0:T(8,128)(2,1)S(1)}, bf16[32,384]{1,0:T(8,128)(2,1)S(1)}, u32[]{:S(2)}, u32[]{:S(2)}) collective-permute-start(bf16[32,384]{1,0:T(8,128)(2,1)S(1)} %shard_map.132), channel_id=1, source_target_pairs={{0,9},{1,8},{2,11},{3,10},{4,14},{5,15},{6,12},{7,13},{8,1},{9,0},... | collective-permute-start | bytes 73736 | tf_op jit(solution)/shard_map/ppermute | solution.py:271
  6.6 2.5 %collective-permute-start.2 = (bf16[32,384]{1,0:T(8,128)(2,1)S(1)}, bf16[32,384]{1,0:T(8,128)(2,1)S(1)}, u32[]{:S(2)}, u32[]{:S(2)}) collective-permute-start(bf16[32,384]{1,0:T(8,128)(2,1)S(1)} %shard_map.132), channel_id=1, source_target_pairs={{0,3},{1,2},{2,1},{3,0},{4,15},{5,14},{6,13},{7,12},{8,11},{9,10},... | collective-permute-start | bytes 73736 | tf_op jit(solution)/shard_map/ppermute | solution.py:271
  9.1 0.7 %collective-permute-start.1 = (bf16[32,384]{1,0:T(8,128)(2,1)S(1)}, bf16[32,384]{1,0:T(8,128)(2,1)S(1)}, u32[]{:S(2)}, u32[]{:S(2)}) collective-permute-start(bf16[32,384]{1,0:T(8,128)(2,1)S(1)} %shard_map.132), channel_id=1, source_target_pairs={{0,1},{1,0},{2,3},{3,2},{4,6},{5,7},{6,4},{7,5},{8,9},{9,8},{10,11... | collective-permute-start | bytes 73736 | tf_op jit(solution)/shard_map/ppermute | solution.py:271
  9.8 0.0 collective-permute-done.4
  9.8 2.5 %collective-permute-done.2.refs_1_ = bf16[32,384]{1,0:T(8,128)(2,1)S(1)} collective-permute-done((bf16[32,384]{1,0:T(8,128)(2,1)S(1)}, bf16[32,384]{1,0:T(8,128)(2,1)S(1)}, u32[]{:S(2)}, u32[]{:S(2)}) %collective-permute-start.2) | collective-permute-done | bytes 24608 | tf_op jit(solution)/shard_map/ppermute | solution.py:271
  12.3 0.7 %collective-permute-done.1.refs_0_ = bf16[32,384]{1,0:T(8,128)(2,1)S(1)} collective-permute-done((bf16[32,384]{1,0:T(8,128)(2,1)S(1)}, bf16[32,384]{1,0:T(8,128)(2,1)S(1)}, u32[]{:S(2)}, u32[]{:S(2)}) %collective-permute-start.1) | collective-permute-done | bytes 24608 | tf_op jit(solution)/shard_map/ppermute | solution.py:271
  12.9 0.5 %collective-permute-start.3 = (bf16[64,384]{1,0:T(8,128)(2,1)S(1)}, bf16[64,384]{1,0:T(8,128)(2,1)S(1)}, u32[]{:S(2)}, u32[]{:S(2)}) collective-permute-start(bf16[64,384]{1,0:T(8,128)(2,1)S(1)} %shard_map.133.refs_0_.got), channel_id=1, source_target_pairs={{0,4},{1,5},{2,6},{3,7},{4,0},{5,1},{6,2},{7,3},{8,12},{9,13},{10,... | collective-permute-start | bytes 147464 | tf_op jit(solution)/shard_map/ppermute | solution.py:271
  13.5 0.1 collective-permute-start.6
  14.2 1.3 %shard_map.131 = (bf16[768,128]{1,0:T(8,128)(2,1)S(1)}, bf16[768,128]{1,0:T(8,128)(2,1)S(1)}, f32[128,1]{1,0:T(8,128)S(1)}, f32[384]{0:T(512)S(1)}, bf16[384,384...) custom-call(bf16[128,384]{1,0:T(8,128)(2,1)S(1)} %get-tuple-element.32.queries, ...), custom_call_target="tpu_custom_call" | custom-call | tf_op jit(solution)/shard_map/pallas_call | solution.py:244
  15.5 1.2 %shard_map.134 = (f32[16,384]{1,0:T(8,128)S(1)}, bf16[48,384]{1,0:T(8,128)(2,1)S(1)}, f32[64,384]{1,0:T(8,128)S(1)}, bf16[128,384]{1,0:T(8,128)(2,1)S(1)}, bf16[128,384]{1,0:T(8,128)(2,1)S(1)}) custom-call(s32[1,128]{1,0:T(1,128)S(1)} %get-tuple-element.38.kind, bf16[768,128]{1,0:T(8,128)(2,1)S(1)} %get-tuple-element.39.heads, ...), custom_call_target="tpu_custom_call" | custom-call | tf_op jit(solution)/shard_map/pallas_call | solution.py:244
  16.6 1.2 %shard_map.135 = (bf16[80,384]{1,0:T(8,128)(2,1)S(1)}, f32[80,384]{1,0:T(8,128)S(1)}, bf16[128,384]{1,0:T(8,128)(2,1)S(1)}, bf16[128,384]{1,0:T(8,128)(2,1)S(1)}) custom-call(s32[1,128]{1,0:T(1,128)S(1)} %get-tuple-element.38.kind, bf16[768,128]{1,0:T(8,128)(2,1)S(1)} %get-tuple-element.39.heads, bf16[768,128]{1,0:T(8,128)(2,1)S(1)} %get-tuple-element.40.grads, ...), custom_call_target="tpu_custom_call" | custom-call | tf_op jit(solution)/shard_map/pallas_call | solution.py:244
  17.8 0.6 %collective-permute-start.9 = (bf16[80,384]{1,0:T(8,128)(2,1)S(1)}, bf16[80,384]{1,0:T(8,128)(2,1)S(1)}, u32[]{:S(2)}, u32[]{:S(2)}) collective-permute-start(bf16[80,384]{1,0:T(8,128)(2,1)S(1)} %get-tuple-element.54), channel_id=1, source_target_pairs={{0,4},{1,5},{2,6},{3,7},{4,0},{5,1},{6,2},{7,3},{8,12},{9,13},{10,... | collective-permute-start | bytes 184328 | tf_op jit(solution)/shard_map/ppermute | solution.py:271
  18.4 0.1 collective-permute-start.7
  18.5 1.1 %collective-permute-done.7.got = bf16[48,384]{1,0:T(8,128)(2,1)S(1)} collective-permute-done((bf16[48,384]{1,0:T(8,128)(2,1)S(1)}, bf16[48,384]{1,0:T(8,128)(2,1)S(1)}, u32[]{:S(2)}, u32[]{:S(2)}) %collective-permute-start.7) | collective-permute-done | bytes 36896 | tf_op jit(solution)/shard_map/ppermute | solution.py:271
  19.6 0.4 %collective-permute-start.8 = (bf16[32,384]{1,0:T(8,128)(2,1)S(1)}, bf16[32,384]{1,0:T(8,128)(2,1)S(1)}, u32[]{:S(2)}, u32[]{:S(2)}) collective-permute-start(bf16[32,384]{1,0:T(8,128)(2,1)S(1)} %get-tuple-element.52), channel_id=1, source_target_pairs={{0,1},{1,0},{2,3},{3,2},{4,6},{5,7},{6,4},{7,5},{8,9},{9,8},{10,11... | collective-permute-start | bytes 73736 | tf_op jit(solution)/shard_map/ppermute | solution.py:271
  20.0 0.0 collective-permute-done.9.got
  20.0 2.6 %collective-permute-start.10 = (bf16[32,384]{1,0:T(8,128)(2,1)S(1)}, bf16[32,384]{1,0:T(8,128)(2,1)S(1)}, u32[]{:S(2)}, u32[]{:S(2)}) collective-permute-start(bf16[32,384]{1,0:T(8,128)(2,1)S(1)} %get-tuple-element.55), channel_id=1, source_target_pairs={{0,3},{1,2},{2,1},{3,0},{4,15},{5,14},{6,13},{7,12},{8,11},{9,10},... | collective-permute-start | bytes 73736 | tf_op jit(solution)/shard_map/ppermute | solution.py:271
  22.6 0.8 %collective-permute-start.11 = (bf16[32,384]{1,0:T(8,128)(2,1)S(1)}, bf16[32,384]{1,0:T(8,128)(2,1)S(1)}, u32[]{:S(2)}, u32[]{:S(2)}) collective-permute-start(bf16[32,384]{1,0:T(8,128)(2,1)S(1)} %get-tuple-element.56), channel_id=1, source_target_pairs={{0,9},{1,8},{2,11},{3,10},{4,14},{5,15},{6,12},{7,13},{8,1},{9,0},... | collective-permute-start | bytes 73736 | tf_op jit(solution)/shard_map/ppermute | solution.py:271
  23.4 1.3 %collective-permute-start.13 = (bf16[16,384]{1,0:T(8,128)(2,1)S(1)}, bf16[16,384]{1,0:T(8,128)(2,1)S(1)}, u32[]{:S(2)}, u32[]{:S(2)}) collective-permute-start(bf16[16,384]{1,0:T(8,128)(2,1)S(1)} %get-tuple-element.60), channel_id=1, source_target_pairs={{0,8},{1,9},{2,10},{3,11},{4,12},{5,13},{6,14},{7,15},{8,0},{9,1},... | collective-permute-start | bytes 36872 | tf_op jit(solution)/shard_map/ppermute | solution.py:271
  24.7 0.0 collective-permute-done.8.refs_0_
  24.7 1.2 %collective-permute-done.10.refs_1_ = bf16[32,384]{1,0:T(8,128)(2,1)S(1)} collective-permute-done((bf16[32,384]{1,0:T(8,128)(2,1)S(1)}, bf16[32,384]{1,0:T(8,128)(2,1)S(1)}, u32[]{:S(2)}, u32[]{:S(2)}) %collective-permute-start.10) | collective-permute-done | bytes 24608 | tf_op jit(solution)/shard_map/ppermute | solution.py:271
  26.0 1.5 %collective-permute-done.11.refs_2_ = bf16[32,384]{1,0:T(8,128)(2,1)S(1)} collective-permute-done((bf16[32,384]{1,0:T(8,128)(2,1)S(1)}, bf16[32,384]{1,0:T(8,128)(2,1)S(1)}, u32[]{:S(2)}, u32[]{:S(2)}) %collective-permute-start.11) | collective-permute-done | bytes 24608 | tf_op jit(solution)/shard_map/ppermute | solution.py:271
  27.5 0.5 %collective-permute-start.12 = (bf16[16,384]{1,0:T(8,128)(2,1)S(1)}, bf16[16,384]{1,0:T(8,128)(2,1)S(1)}, u32[]{:S(2)}, u32[]{:S(2)}) collective-permute-start(bf16[16,384]{1,0:T(8,128)(2,1)S(1)} %get-tuple-element.59), channel_id=1, source_target_pairs={{0,4},{1,5},{2,6},{3,7},{4,0},{5,1},{6,2},{7,3},{8,12},{9,13},{10,... | collective-permute-start | bytes 36872 | tf_op jit(solution)/shard_map/ppermute | solution.py:271
  28.0 1.1 %shard_map.137 = f32[128,384]{1,0:T(8,128)} custom-call(f32[128,1]{1,0:T(8,128)S(1)} %get-tuple-element.37.live, bf16[128,384]{1,0:T(8,128)(2,1)S(1)} %get-tuple-element.32.queries, bf16[128,384]{1,0:T(8,128)(2,1)S(1)} %get-tuple-element.33.cot, bf16[128,384]{1,0:T(8,128)(2,1)S(1)} %get-tuple-element.48.near, bf16[128,384]{1,0:T(8,128)(2,1)S(1)} %get-tuple-element.49.far, ...), custom_call_target="tpu_custom_call" | custom-call | tf_op jit(solution)/shard_map/pallas_call | solution.py:244
  29.1 0.9 %shard_map.136 = bf16[128,384]{1,0:T(8,128)(2,1)} custom-call(f32[128,1]{1,0:T(8,128)S(1)} %get-tuple-element.37.live, bf16[128,384]{1,0:T(8,128)(2,1)S(1)} %get-tuple-element.32.queries, bf16[128,384]{1,0:T(8,128)(2,1)S(1)} %get-tuple-element.45.near, bf16[128,384]{1,0:T(8,128)(2,1)S(1)} %get-tuple-element.47.far, bf16[384,384]{1,0:T(8,128)(2,1)S(1)} %get-tuple-element.36.w_out), custom_call_target="tpu_custom_call" | custom-call | tf_op jit(solution)/shard_map/pallas_call | solution.py:244
  29.9 0.0 collective-permute-done.13.across
  29.9 0.0 collective-permute-done.12.got
  30.0 0.9 %shard_map.141 = f32[16,384]{1,0:T(8,128)} custom-call(bf16[16,384]{1,0:T(8,128)(2,1)S(1)} %get-tuple-element.44.own.anchors, f32[16,384]{1,0:T(8,128)S(1)} %get-tuple-element.58.own, bf16[16,384]{1,0:T(8,128)(2,1)S(1)} %collective-permute-done.12.got, bf16[16,384]{1,0:T(8,128)(2,1)S(1)} %collective-permute-done.13.across, f32[384]{0:T(512)S(1)} %get-tuple-element.41.gain), custom_call_target="tpu_custom_call" | custom-call | tf_op jit(solution)/shard_map/pallas_call | solution.py:244
  (10 shorter events, 0.1 us)
Async XLA Ops:
  0.6 4.4 %collective-permute-start = (bf16[16,384]{1,0:T(8,128)(2,1)}, bf16[16,384]{1,0:T(8,128)(2,1)S(1)}, u32[]{:S(2)}, u32[]{:S(2)}) collective-permute-start(bf16[16,384]{1,0:T(8,128)(2,1)} %refs_0_.2), channel_id=1, source_target_pairs={{0,4},{1,5},{2,6},{3,7},{4,0},{5,1},{6,2},{7,3},{8,12},{9,13},{10,... | collective-permute-start | bytes 36872 | tf_op jit(solution)/shard_map/ppermute | solution.py:271
  1.2 8.6 %collective-permute-start.4 = (bf16[16,384]{1,0:T(8,128)(2,1)}, bf16[16,384]{1,0:T(8,128)(2,1)S(1)}, u32[]{:S(2)}, u32[]{:S(2)}) collective-permute-start(bf16[16,384]{1,0:T(8,128)(2,1)} %refs_0_.2), channel_id=1, source_target_pairs={{0,8},{1,9},{2,10},{3,11},{4,12},{5,13},{6,14},{7,15},{8,0},{9,1},... | collective-permute-start | bytes 36872 | tf_op jit(solution)/shard_map/ppermute | solution.py:271
  5.0 8.4 %collective-permute-start.5 = (bf16[32,384]{1,0:T(8,128)(2,1)S(1)}, bf16[32,384]{1,0:T(8,128)(2,1)S(1)}, u32[]{:S(2)}, u32[]{:S(2)}) collective-permute-start(bf16[32,384]{1,0:T(8,128)(2,1)S(1)} %shard_map.132), channel_id=1, source_target_pairs={{0,9},{1,8},{2,11},{3,10},{4,14},{5,15},{6,12},{7,13},{8,1},{9,0},... | collective-permute-start | bytes 73736 | tf_op jit(solution)/shard_map/ppermute | solution.py:271
  6.6 5.6 %collective-permute-start.2 = (bf16[32,384]{1,0:T(8,128)(2,1)S(1)}, bf16[32,384]{1,0:T(8,128)(2,1)S(1)}, u32[]{:S(2)}, u32[]{:S(2)}) collective-permute-start(bf16[32,384]{1,0:T(8,128)(2,1)S(1)} %shard_map.132), channel_id=1, source_target_pairs={{0,3},{1,2},{2,1},{3,0},{4,15},{5,14},{6,13},{7,12},{8,11},{9,10},... | collective-permute-start | bytes 73736 | tf_op jit(solution)/shard_map/ppermute | solution.py:271
  9.1 3.8 %collective-permute-start.1 = (bf16[32,384]{1,0:T(8,128)(2,1)S(1)}, bf16[32,384]{1,0:T(8,128)(2,1)S(1)}, u32[]{:S(2)}, u32[]{:S(2)}) collective-permute-start(bf16[32,384]{1,0:T(8,128)(2,1)S(1)} %shard_map.132), channel_id=1, source_target_pairs={{0,1},{1,0},{2,3},{3,2},{4,6},{5,7},{6,4},{7,5},{8,9},{9,8},{10,11... | collective-permute-start | bytes 73736 | tf_op jit(solution)/shard_map/ppermute | solution.py:271
  12.9 2.5 %collective-permute-start.3 = (bf16[64,384]{1,0:T(8,128)(2,1)S(1)}, bf16[64,384]{1,0:T(8,128)(2,1)S(1)}, u32[]{:S(2)}, u32[]{:S(2)}) collective-permute-start(bf16[64,384]{1,0:T(8,128)(2,1)S(1)} %shard_map.133.refs_0_.got), channel_id=1, source_target_pairs={{0,4},{1,5},{2,6},{3,7},{4,0},{5,1},{6,2},{7,3},{8,12},{9,13},{10,... | collective-permute-start | bytes 147464 | tf_op jit(solution)/shard_map/ppermute | solution.py:271
  13.5 3.2 %collective-permute-start.6 = (bf16[48,384]{1,0:T(8,128)(2,1)S(1)}, bf16[48,384]{1,0:T(8,128)(2,1)S(1)}, u32[]{:S(2)}, u32[]{:S(2)}) collective-permute-start(bf16[48,384]{1,0:T(8,128)(2,1)S(1)} %constant_dynamic-update-slice_fusion.got_far), channel_id=1, source_target_pairs={{0,4},{1,5},{2,6},{3,7},{4,0},{5,1},{6,2},{7,3},{8,12},{9,13},{10,... | collective-permute-start | bytes 110600 | tf_op jit(solution)/shard_map/ppermute | solution.py:271
  17.8 2.2 %collective-permute-start.9 = (bf16[80,384]{1,0:T(8,128)(2,1)S(1)}, bf16[80,384]{1,0:T(8,128)(2,1)S(1)}, u32[]{:S(2)}, u32[]{:S(2)}) collective-permute-start(bf16[80,384]{1,0:T(8,128)(2,1)S(1)} %get-tuple-element.54), channel_id=1, source_target_pairs={{0,4},{1,5},{2,6},{3,7},{4,0},{5,1},{6,2},{7,3},{8,12},{9,13},{10,... | collective-permute-start | bytes 184328 | tf_op jit(solution)/shard_map/ppermute | solution.py:271
  18.4 1.2 %collective-permute-start.7 = (bf16[48,384]{1,0:T(8,128)(2,1)S(1)}, bf16[48,384]{1,0:T(8,128)(2,1)S(1)}, u32[]{:S(2)}, u32[]{:S(2)}) collective-permute-start(bf16[48,384]{1,0:T(8,128)(2,1)S(1)} %get-tuple-element.51), channel_id=1, source_target_pairs={{0,4},{1,5},{2,6},{3,7},{4,0},{5,1},{6,2},{7,3},{8,12},{9,13},{10,... | collective-permute-start | bytes 110600 | tf_op jit(solution)/shard_map/ppermute | solution.py:271
  19.6 5.1 %collective-permute-start.8 = (bf16[32,384]{1,0:T(8,128)(2,1)S(1)}, bf16[32,384]{1,0:T(8,128)(2,1)S(1)}, u32[]{:S(2)}, u32[]{:S(2)}) collective-permute-start(bf16[32,384]{1,0:T(8,128)(2,1)S(1)} %get-tuple-element.52), channel_id=1, source_target_pairs={{0,1},{1,0},{2,3},{3,2},{4,6},{5,7},{6,4},{7,5},{8,9},{9,8},{10,11... | collective-permute-start | bytes 73736 | tf_op jit(solution)/shard_map/ppermute | solution.py:271
  20.0 5.9 %collective-permute-start.10 = (bf16[32,384]{1,0:T(8,128)(2,1)S(1)}, bf16[32,384]{1,0:T(8,128)(2,1)S(1)}, u32[]{:S(2)}, u32[]{:S(2)}) collective-permute-start(bf16[32,384]{1,0:T(8,128)(2,1)S(1)} %get-tuple-element.55), channel_id=1, source_target_pairs={{0,3},{1,2},{2,1},{3,0},{4,15},{5,14},{6,13},{7,12},{8,11},{9,10},... | collective-permute-start | bytes 73736 | tf_op jit(solution)/shard_map/ppermute | solution.py:271
  22.6 4.8 %collective-permute-start.11 = (bf16[32,384]{1,0:T(8,128)(2,1)S(1)}, bf16[32,384]{1,0:T(8,128)(2,1)S(1)}, u32[]{:S(2)}, u32[]{:S(2)}) collective-permute-start(bf16[32,384]{1,0:T(8,128)(2,1)S(1)} %get-tuple-element.56), channel_id=1, source_target_pairs={{0,9},{1,8},{2,11},{3,10},{4,14},{5,15},{6,12},{7,13},{8,1},{9,0},... | collective-permute-start | bytes 73736 | tf_op jit(solution)/shard_map/ppermute | solution.py:271
  23.4 6.5 %collective-permute-start.13 = (bf16[16,384]{1,0:T(8,128)(2,1)S(1)}, bf16[16,384]{1,0:T(8,128)(2,1)S(1)}, u32[]{:S(2)}, u32[]{:S(2)}) collective-permute-start(bf16[16,384]{1,0:T(8,128)(2,1)S(1)} %get-tuple-element.60), channel_id=1, source_target_pairs={{0,8},{1,9},{2,10},{3,11},{4,12},{5,13},{6,14},{7,15},{8,0},{9,1},... | collective-permute-start | bytes 36872 | tf_op jit(solution)/shard_map/ppermute | solution.py:271
  27.5 2.5 %collective-permute-start.12 = (bf16[16,384]{1,0:T(8,128)(2,1)S(1)}, bf16[16,384]{1,0:T(8,128)(2,1)S(1)}, u32[]{:S(2)}, u32[]{:S(2)}) collective-permute-start(bf16[16,384]{1,0:T(8,128)(2,1)S(1)} %get-tuple-element.59), channel_id=1, source_target_pairs={{0,4},{1,5},{2,6},{3,7},{4,0},{5,1},{6,2},{7,3},{8,12},{9,13},{10,... | collective-permute-start | bytes 36872 | tf_op jit(solution)/shard_map/ppermute | solution.py:271
